TPU v7x, 512 devices: a whole 4x4x16 slice. The times are simulated.
512 devices in a mesh: tile: 16 (over x, y_hi, core), pos: 32 (over z, y_lo).
Axes of the slice: x: 4, y: 4 (y_hi: 2, y_lo: 2; y = y_hi * 2 + y_lo), z: 16, core: 2. Of those that a mesh axis runs over, the one named last changes fastest.
Arguments:
- patterns: bfloat16 [8192, 128, 128], P(('tile', 'pos')), may hold values from 0 to 2
- coords: int32 [8192, 2], P(('tile', 'pos')), may hold values from 0 to 2047, as said below
- send_slots: int32 [512, 16, 2], P(('tile', 'pos')), may hold values from 0 to 15, as said below
- send_counts: int32 [512, 16], P(('tile', 'pos')), may hold values from 0 to 2, as said below
- object_real: float32 [2, 256, 2048], P(None, 'pos', 'tile'), may hold values from 0.5 to 1.5
- object_imag: float32 [2, 256, 2048], P(None, 'pos', 'tile'), may hold values from -2 to 2
- probe_real: float32 [128, 128], replicated, may hold values from -6 to 6
- probe_imag: float32 [128, 128], replicated, may hold values from -6 to 6
Outputs:
- grad_real: float32 [2, 256, 2048], P(None, 'pos', 'tile')
- grad_imag: float32 [2, 256, 2048], P(None, 'pos', 'tile')
Inputs may be any that keep to these rules, and one draw needn't show every extreme that they name: `coords`: A pattern listed under tile d has its column in [d * 128, (d + 1) * 128); rows are at most 128. `send_slots`: for each block, the live entries over all tiles list each of its 16 patterns exactly once; entries from the count on are arbitrary block-local indices. `send_counts`: for each block the counts sum to 16.
All inputs are finite; a program needn't handle non-finite values.
Results may differ from a plain program's by a relative error of at most 0.018.
Values may be sent and summed in bfloat16 or wider, within the bound.
No kernel may reach another device: no remote copies, remote signals or barrier semaphores. Data moves between devices by JAX's collectives and lax.ppermute only.
A program may use at most 64 MiB of HBM per device.

v0:
```python
import math

import jax
import jax.numpy as jnp
from jax import lax
from jax.sharding import PartitionSpec as P


def side_by_side(arrays, axis, split_dim, concat_dim, along):
    columns = [a.reshape(*a.shape[:along], -1) for a in arrays]
    both = jnp.concatenate(columns, axis=along)
    result, at, done = (
        lax.all_to_all(both, axis, split_axis=split_dim, concat_axis=concat_dim, tiled=True),
        0,
        [],
    )
    for a, column in zip(arrays, columns):
        slab = result[..., at : at + column.shape[along]]
        done.append(slab.reshape(*slab.shape[:along], *a.shape[along:]))
        at += column.shape[along]
    return tuple(done)


def joined_along(pieces, dim):
    dims = list(pieces.shape[1:])
    dims[dim] *= pieces.shape[0]
    return jnp.moveaxis(pieces, 0, dim).reshape(dims)


def sent_to_all(shard, axis):
    length = lax.axis_size(axis)
    return lax.all_to_all(
        jnp.broadcast_to(shard[None], (length, *shard.shape)), axis, 0, 0, tiled=True
    )


def collect(shard, axis, dim):
    return joined_along(sent_to_all(shard, axis), dim)


def side_by_side_2(arrays, axis, dim, along):
    ends, at = ([], 0)
    for a in arrays[:-1]:
        at += a.shape[along]
        ends.append(at)
    both = jnp.concatenate(arrays, axis=along)
    return tuple(jnp.split(collect(both, axis, dim), ends, axis=along))


def shifted(value, axis, steps):
    count = lax.axis_size(axis)
    first, last = (max(0, -steps), min(count, count - steps))
    return lax.ppermute(value, axis, [(source, source + steps) for source in range(first, last)])


def split_up(shard, dim, length):
    before, after = (shard.shape[:dim], shard.shape[dim + 1 :])
    return jnp.moveaxis(shard.reshape(*before, length, -1, *after), dim, 0)


def sent_and_summed(shard, axis, dim):
    length = lax.axis_size(axis)
    pieces = lax.all_to_all(split_up(shard, dim, length), axis, 0, 0, tiled=True)
    return jnp.sum(pieces.astype(jnp.float32), axis=0)


def build_tables(edge_len):
    indices = jnp.arange(edge_len, dtype=jnp.int32)
    products = indices[:, None] * indices[None, :] % edge_len
    phases = products.astype(jnp.float32) * (2.0 * math.pi / edge_len)
    unit_norm = 1.0 / math.sqrt(edge_len)
    wave_re = jnp.cos(phases) * unit_norm
    wave_im = jnp.sin(phases) * unit_norm
    centred = jnp.where(indices < edge_len // 2, indices, indices - edge_len).astype(jnp.float32)
    chirp = 0.5 * math.pi * centred * centred / edge_len
    kern_re = jnp.cos(chirp)
    kern_im = -jnp.sin(chirp)
    scaled_re = wave_re * kern_re[None, :] - wave_im * kern_im[None, :]
    scaled_im = wave_re * kern_im[None, :] + wave_im * kern_re[None, :]
    highest = lax.Precision.HIGHEST
    fres_re = jnp.dot(scaled_re, wave_re.T, precision=highest) + jnp.dot(
        scaled_im, wave_im.T, precision=highest
    )
    fres_im = jnp.dot(scaled_im, wave_re.T, precision=highest) - jnp.dot(
        scaled_re, wave_im.T, precision=highest
    )
    fq_re = fres_re.astype(jnp.bfloat16)
    fq_im = fres_im.astype(jnp.bfloat16)
    dft_re = wave_re.astype(jnp.bfloat16)
    dft_im = (-wave_im).astype(jnp.bfloat16)
    return (fq_re, fq_im, fq_re.T, fq_im.T, dft_re, dft_im)


def left_mul(mat_re, mat_im, data_re, data_im):

    def product(a, x):
        return jnp.einsum("jk,nkl->njl", a, x, preferred_element_type=jnp.float32)

    return (
        product(mat_re, data_re) - product(mat_im, data_im),
        product(mat_re, data_im) + product(mat_im, data_re),
    )


def right_mul(data_re, data_im, mat_re, mat_im):

    def product(x, a):
        return jnp.einsum("njk,kl->njl", x, a, preferred_element_type=jnp.float32)

    return (
        product(data_re, mat_re) - product(data_im, mat_im),
        product(data_re, mat_im) + product(data_im, mat_re),
    )


def transform(data_re, data_im, left_re, left_im, right_re, right_im):
    half_re, half_im = left_mul(left_re, left_im, data_re, data_im)
    return right_mul(half_re.astype(jnp.bfloat16), half_im.astype(jnp.bfloat16), right_re, right_im)


def slot_gradients(windows, probe_real, probe_imag, measured, weights, tables):
    fq_re, fq_im, fqt_re, fqt_im, dft_re, dft_im = tables
    slices = windows.shape[2]
    shape = (windows.shape[0],) + probe_real.shape
    wave_re = jnp.broadcast_to(probe_real, shape)
    wave_im = jnp.broadcast_to(probe_imag, shape)
    incident = []
    for s in range(slices):
        incident.append((wave_re, wave_im))
        slab_re = windows[:, 0, s]
        slab_im = windows[:, 1, s]
        exit_re = (wave_re * slab_re - wave_im * slab_im).astype(jnp.bfloat16)
        exit_im = (wave_re * slab_im + wave_im * slab_re).astype(jnp.bfloat16)
        if s < slices - 1:
            wave_re, wave_im = transform(exit_re, exit_im, fq_re, fq_im, fqt_re, fqt_im)
        else:
            far_re, far_im = transform(exit_re, exit_im, dft_re, dft_im, dft_re, dft_im)
    excess = far_re * far_re + far_im * far_im - measured.astype(jnp.float32)
    weighted = weights[:, None, None] * excess
    chi_re = (weighted * far_re).astype(jnp.bfloat16)
    chi_im = (weighted * far_im).astype(jnp.bfloat16)
    back_re, back_im = transform(chi_re, chi_im, dft_re, -dft_im, dft_re, -dft_im)
    slice_grads = [None] * slices
    for s in reversed(range(slices)):
        wave_re, wave_im = incident[s]
        slice_grads[s] = (
            wave_re * back_re + wave_im * back_im,
            wave_re * back_im - wave_im * back_re,
        )
        if s > 0:
            slab_re = windows[:, 0, s]
            slab_im = windows[:, 1, s]
            carry_re = (slab_re * back_re + slab_im * back_im).astype(jnp.bfloat16)
            carry_im = (slab_re * back_im - slab_im * back_re).astype(jnp.bfloat16)
            back_re, back_im = transform(carry_re, carry_im, fqt_re, -fqt_im, fq_re, -fq_im)
    real_part = jnp.stack([pair[0] for pair in slice_grads], 1)
    imag_part = jnp.stack([pair[1] for pair in slice_grads], 1)
    return jnp.stack([real_part, imag_part], 1)


def body(
    patterns, coords, send_slots, send_counts, object_real, object_imag, probe_real, probe_imag
):
    edge_len = probe_real.shape[0]
    tile_width = object_real.shape[2]
    slices = object_real.shape[0]
    n_tile = lax.axis_size("tile")
    n_pos = lax.axis_size("pos")
    per_source = patterns.shape[0]
    slot_cap = send_slots.shape[2]
    slot_count = n_tile * slot_cap
    listed = send_slots[0].reshape(-1)
    out_patterns = jnp.take(patterns, listed, axis=0).reshape(n_tile, slot_cap, edge_len, edge_len)
    out_corners = jnp.take(coords, listed, axis=0).reshape(n_tile, slot_cap, 2)
    live_flag = (jnp.arange(slot_cap, dtype=jnp.int32)[None, :] < send_counts[0][:, None]).astype(
        jnp.int32
    )
    got_patterns, got_corners, got_live = (
        lax.all_to_all(out_patterns, "tile", split_axis=0, concat_axis=0, tiled=True),
        *side_by_side((out_corners, live_flag), "tile", 0, 0, 2),
    )
    measured = got_patterns.reshape(slot_count, edge_len, edge_len)
    positions = got_corners.reshape(slot_count, 2)
    weights = got_live.reshape(slot_count).astype(jnp.float32)
    whole_re, whole_im = side_by_side_2((object_real, object_imag), "pos", 1, 0)
    rim_re, rim_im = (
        shifted(whole_re.astype(jnp.bfloat16), "tile", -1).astype(whole_re.dtype),
        shifted(whole_im.astype(jnp.bfloat16), "tile", -1).astype(whole_im.dtype),
    )
    ext_re = jnp.concatenate([whole_re, rim_re], 2)
    ext_im = jnp.concatenate([whole_im, rim_im], 2)
    extended = jnp.stack([ext_re, ext_im])
    all_rows = extended.shape[2]
    tile_index = lax.axis_index("tile")
    row_start = jnp.clip(positions[:, 0], 0, all_rows - edge_len).astype(jnp.int32)
    col_start = jnp.clip(positions[:, 1] - tile_index * tile_width, 0, tile_width).astype(jnp.int32)
    tables = build_tables(edge_len)
    anchor = jnp.int32(0)
    group_len = 8

    def cut_window(row_at, col_at):
        return lax.dynamic_slice(
            extended, (anchor, anchor, row_at, col_at), (2, slices, edge_len, edge_len)
        )

    def run_group(b, running):
        first = b * group_len
        rows_here = lax.dynamic_slice_in_dim(row_start, first, group_len)
        cols_here = lax.dynamic_slice_in_dim(col_start, first, group_len)
        windows = jax.vmap(cut_window)(rows_here, cols_here)
        slot_terms = slot_gradients(
            windows,
            probe_real,
            probe_imag,
            lax.dynamic_slice_in_dim(measured, first, group_len),
            lax.dynamic_slice_in_dim(weights, first, group_len),
            tables,
        )

        def add_window(k, summed):
            start = (anchor, anchor, rows_here[k], cols_here[k])
            current = lax.dynamic_slice(summed, start, (2, slices, edge_len, edge_len))
            return lax.dynamic_update_slice(summed, current + slot_terms[k], start)

        return lax.fori_loop(0, group_len, add_window, running)

    running = lax.fori_loop(
        0, slot_count // group_len, run_group, jnp.zeros(extended.shape, jnp.float32)
    )
    spill = shifted(running[:, :, :, tile_width:].astype(jnp.bfloat16), "tile", 1).astype(
        jnp.float32
    )
    owned = running[:, :, :, :tile_width]
    owned = owned.at[:, :, :, :edge_len].add(spill)
    share = sent_and_summed(owned.astype(jnp.bfloat16), "pos", 2)
    share = share * (1.0 / math.sqrt(per_source * n_pos))
    return (share[0], share[1])


def solution(mesh):
    in_specs = (
        P(("tile", "pos"), None, None),
        P(("tile", "pos"), None),
        P(("tile", "pos"), None, None),
        P(("tile", "pos"), None),
        P(None, "pos", "tile"),
        P(None, "pos", "tile"),
        P(),
        P(),
    )
    out_specs = (P(None, "pos", "tile"), P(None, "pos", "tile"))
    return jax.shard_map(body, mesh=mesh, in_specs=in_specs, out_specs=out_specs, check_vma=False)
```

profile of v0, /device:TPU:6, one launch (start us, length us, event | category | flops | bytes accessed | tf_op | source)
XLA Modules:
  0.0 611.3 jit_solution(12424330342253916811)
XLA Ops:
  5.4 9.2 %all-to-all-start = ((s32[16,2,3]{2,1,0:T(2,128)}), s32[16,2,3]{2,1,0:T(2,128)S(1)}, u32[]{:S(2)}, u32[]{:S(2)}) async-start(s32[16,2,3]{2,1,0:T(2,128)} %copy.239), calls=%async_computation | async-start | bytes 32768 | tf_op jit(solution)/shard_map/all_to_all | solution.py:13
  15.3 4.9 all-to-all-done
  21.0 13.9 %all-to-all-start.1 = ((f32[32,4,8,128]{3,2,1,0:T(8,128)}), f32[32,4,8,128]{3,2,1,0:T(8,128)S(1)}, u32[]{:S(2)}, u32[]{:S(2)}) async-start(f32[32,4,8,128]{3,2,1,0:T(8,128)} %broadcast_in_dim.74), calls=%async_computation.1 | async-start | bytes 1048576 | tf_op jit(solution)/shard_map/all_to_all | solution.py:32
  39.4 28.7 %all-to-all-done.1 = f32[32,4,8,128]{3,2,1,0:T(8,128)S(1)} async-done(((f32[32,4,8,128]{3,2,1,0:T(8,128)}), f32[32,4,8,128]{3,2,1,0:T(8,128)S(1)}, u32[]{:S(2)}, u32[]{:S(2)}) %all-to-all-start.1) | async-done | bytes 524320 | tf_op jit(solution)/shard_map/all_to_all | solution.py:32
  68.2 6.2 %all-to-all-start.2 = ((bf16[16,2,128,128]{3,2,1,0:T(8,128)(2,1)}), bf16[16,2,128,128]{3,2,1,0:T(8,128)(2,1)}, u32[]{:S(2)}, u32[]{:S(2)}) async-start(bf16[16,2,128,128]{3,2,1,0:T(8,128)(2,1)} %broadcast_select_fusion), calls=%async_computation.2 | async-start | bytes 2097152 | tf_op jit(solution)/shard_map/all_to_all | solution.py:179
  74.9 4.9 collective-permute-start
  79.8 2.5 collective-permute-start.1
  82.3 6.1 %collective-permute-done = bf16[2,256,128]{2,1,0:T(8,128)(2,1)S(1)} collective-permute-done((bf16[2,256,128]{2,1,0:T(8,128)(2,1)S(1)}, bf16[2,256,128]{2,1,0:T(8,128)(2,1)S(1)}, u32[]{:S(2)}, u32[]{:S(2)}) %collective-permute-start) | collective-permute-done | bytes 131104 | tf_op jit(solution)/shard_map/ppermute | solution.py:53
  92.1 464.4 %while.51 = (s32[]{:T(128)}, f32[2,2,256,256]{3,2,1,0:T(8,128)}, s32[32]{0:T(128)S(1)}, s32[32]{0:T(128)S(1)}, f32[128,128]{1,0:T(8,128)S(1)}, /*index=5*/f32[2,...) while((s32[]{:T(128)}, f32[2,2,256,256]{3,2,1,0:T(8,128)}, ...), condition=%wide.region_3.4_spmd.clone.clone, body=%wide.region_0.3_spmd.clone.clone.sunk | while | flops 1088553088 | bytes 51643620 | solution.py:227
  92.4 24.0 %while.52 = (s32[]{:T(128)}, f32[2,2,256,256]{3,2,1,0:T(8,128)}, s32[8,4]{0,1:T(4,128)S(1)}, f32[8,2,2,128,128]{4,3,0,2,1:T(8,128)S(1)}, s32[]{:T(128)}) while((s32[]{:T(128)}, f32[2,2,256,256]{3,2,1,0:T(8,128)}, s32[8,4]{0,1:T(4,128)S(1)}, f32[8,2,2,128,128]{4,3,0,2,1:T(8,128)S(1)}, s32[]{:T(128)}) %tuple.140), condition=%wide.while_cond.1, body=%wide.while_body.1.sunk | while | flops 2 | bytes 524421 | solution.py:202
  93.0 2.4 bitcast_dynamic-update-slice_fusion.2
  96.0 2.4 bitcast_dynamic-update-slice_fusion.2
  99.0 2.4 bitcast_dynamic-update-slice_fusion.2
  102.0 2.4 bitcast_dynamic-update-slice_fusion.2
  105.0 2.4 bitcast_dynamic-update-slice_fusion.2
  110.9 2.4 bitcast_dynamic-update-slice_fusion.2
  113.9 2.4 bitcast_dynamic-update-slice_fusion.2
  130.2 79.1 %while.53 = (s32[]{:T(128)}, f32[2,2,256,256]{3,2,1,0:T(8,128)}, s32[8]{0:T(128)S(1)}, s32[8]{0:T(128)S(1)}, f32[8,2,2,128,128]{4,3,0,2,1:T(8,128)S(1)}, /*index=5*/s32[]{:T(128)}, s32[]{:T(128)}, s32[]{:T(128)}) while((s32[]{:T(128)}, f32[2,2,256,256]{3,2,1,0:T(8,128)}, s32[8]{0:T(128)S(1)}, s32[8]{0:T(128)S(1)}, ...), condition=%wide.region_2.2_spmd, body=%wide.region_1.1_spmd.sunk | while | flops 65544 | bytes 1310921 | solution.py:225
  136.3 4.3 dynamic_update_slice.8
  146.8 3.5 dynamic_update_slice.8
  156.4 4.2 dynamic_update_slice.8
  166.8 3.2 dynamic_update_slice.8
  176.2 4.3 dynamic_update_slice.8
  186.5 2.8 dynamic_update_slice.8
  195.4 4.2 dynamic_update_slice.8
  205.8 3.5 dynamic_update_slice.8
  209.5 24.0 %while.52 = (s32[]{:T(128)}, f32[2,2,256,256]{3,2,1,0:T(8,128)}, s32[8,4]{0,1:T(4,128)S(1)}, f32[8,2,2,128,128]{4,3,0,2,1:T(8,128)S(1)}, s32[]{:T(128)}) while((s32[]{:T(128)}, f32[2,2,256,256]{3,2,1,0:T(8,128)}, s32[8,4]{0,1:T(4,128)S(1)}, f32[8,2,2,128,128]{4,3,0,2,1:T(8,128)S(1)}, s32[]{:T(128)}) %tuple.140), condition=%wide.while_cond.1, body=%wide.while_body.1.sunk | while | flops 2 | bytes 524421 | solution.py:202
  210.1 2.4 bitcast_dynamic-update-slice_fusion.2
  213.1 2.4 bitcast_dynamic-update-slice_fusion.2
  219.0 2.4 bitcast_dynamic-update-slice_fusion.2
  222.0 2.4 bitcast_dynamic-update-slice_fusion.2
  225.0 2.4 bitcast_dynamic-update-slice_fusion.2
  247.3 76.2 %while.53 = (s32[]{:T(128)}, f32[2,2,256,256]{3,2,1,0:T(8,128)}, s32[8]{0:T(128)S(1)}, s32[8]{0:T(128)S(1)}, f32[8,2,2,128,128]{4,3,0,2,1:T(8,128)S(1)}, /*index=5*/s32[]{:T(128)}, s32[]{:T(128)}, s32[]{:T(128)}) while((s32[]{:T(128)}, f32[2,2,256,256]{3,2,1,0:T(8,128)}, s32[8]{0:T(128)S(1)}, s32[8]{0:T(128)S(1)}, ...), condition=%wide.region_2.2_spmd, body=%wide.region_1.1_spmd.sunk | while | flops 65544 | bytes 1310921 | solution.py:225
  253.4 4.0 dynamic_update_slice.8
  263.5 4.3 dynamic_update_slice.8
  273.9 2.5 dynamic_update_slice.8
  282.6 3.2 dynamic_update_slice.8
  291.9 3.3 dynamic_update_slice.8
  301.3 3.4 dynamic_update_slice.8
  310.9 3.2 dynamic_update_slice.8
  320.3 3.2 dynamic_update_slice.8
  323.7 24.0 %while.52 = (s32[]{:T(128)}, f32[2,2,256,256]{3,2,1,0:T(8,128)}, s32[8,4]{0,1:T(4,128)S(1)}, f32[8,2,2,128,128]{4,3,0,2,1:T(8,128)S(1)}, s32[]{:T(128)}) while((s32[]{:T(128)}, f32[2,2,256,256]{3,2,1,0:T(8,128)}, s32[8,4]{0,1:T(4,128)S(1)}, f32[8,2,2,128,128]{4,3,0,2,1:T(8,128)S(1)}, s32[]{:T(128)}) %tuple.140), condition=%wide.while_cond.1, body=%wide.while_body.1.sunk | while | flops 2 | bytes 524421 | solution.py:202
  361.5 79.1 %while.53 = (s32[]{:T(128)}, f32[2,2,256,256]{3,2,1,0:T(8,128)}, s32[8]{0:T(128)S(1)}, s32[8]{0:T(128)S(1)}, f32[8,2,2,128,128]{4,3,0,2,1:T(8,128)S(1)}, /*index=5*/s32[]{:T(128)}, s32[]{:T(128)}, s32[]{:T(128)}) while((s32[]{:T(128)}, f32[2,2,256,256]{3,2,1,0:T(8,128)}, s32[8]{0:T(128)S(1)}, s32[8]{0:T(128)S(1)}, ...), condition=%wide.region_2.2_spmd, body=%wide.region_1.1_spmd.sunk | while | flops 65544 | bytes 1310921 | solution.py:225
  367.7 3.5 dynamic_update_slice.8
  377.2 2.9 dynamic_update_slice.8
  386.3 4.2 dynamic_update_slice.8
  396.6 4.3 dynamic_update_slice.8
  407.0 4.2 dynamic_update_slice.8
  417.4 4.2 dynamic_update_slice.8
  427.7 3.4 dynamic_update_slice.8
  437.3 3.3 dynamic_update_slice.8
  440.8 23.9 %while.52 = (s32[]{:T(128)}, f32[2,2,256,256]{3,2,1,0:T(8,128)}, s32[8,4]{0,1:T(4,128)S(1)}, f32[8,2,2,128,128]{4,3,0,2,1:T(8,128)S(1)}, s32[]{:T(128)}) while((s32[]{:T(128)}, f32[2,2,256,256]{3,2,1,0:T(8,128)}, s32[8,4]{0,1:T(4,128)S(1)}, f32[8,2,2,128,128]{4,3,0,2,1:T(8,128)S(1)}, s32[]{:T(128)}) %tuple.140), condition=%wide.while_cond.1, body=%wide.while_body.1.sunk | while | flops 2 | bytes 524421 | solution.py:202
  478.5 78.0 %while.53 = (s32[]{:T(128)}, f32[2,2,256,256]{3,2,1,0:T(8,128)}, s32[8]{0:T(128)S(1)}, s32[8]{0:T(128)S(1)}, f32[8,2,2,128,128]{4,3,0,2,1:T(8,128)S(1)}, /*index=5*/s32[]{:T(128)}, s32[]{:T(128)}, s32[]{:T(128)}) while((s32[]{:T(128)}, f32[2,2,256,256]{3,2,1,0:T(8,128)}, s32[8]{0:T(128)S(1)}, s32[8]{0:T(128)S(1)}, ...), condition=%wide.region_2.2_spmd, body=%wide.region_1.1_spmd.sunk | while | flops 65544 | bytes 1310921 | solution.py:225
  484.7 3.3 dynamic_update_slice.8
  494.1 3.3 dynamic_update_slice.8
  503.6 4.3 dynamic_update_slice.8
  514.0 4.2 dynamic_update_slice.8
  524.4 4.3 dynamic_update_slice.8
  534.7 2.9 dynamic_update_slice.8
  543.7 4.0 dynamic_update_slice.8
  553.8 2.7 dynamic_update_slice.8
  557.6 6.6 %collective-permute-start.2 = (bf16[2,2,256,128]{3,2,1,0:T(8,128)(2,1)S(1)}, bf16[2,2,256,128]{3,2,1,0:T(8,128)(2,1)S(1)}, u32[]{:S(2)}, u32[]{:S(2)}) collective-permute-start(bf16[2,2,256,128]{3,2,1,0:T(8,128)(2,1)S(1)} %slice.154), channel_id=1, source_target_pairs={{0,32},{32,64},{64,96},{96,128},{128,160},{160,192},{192,224},{224... | collective-permute-start | bytes 786440 | tf_op jit(solution)/shard_map/ppermute | solution.py:53
  564.3 8.8 %collective-permute-done.2 = bf16[2,2,256,128]{3,2,1,0:T(8,128)(2,1)S(1)} collective-permute-done((bf16[2,2,256,128]{3,2,1,0:T(8,128)(2,1)S(1)}, bf16[2,2,256,128]{3,2,1,0:T(8,128)(2,1)S(1)}, u32[]{:S(2)}, u32[]{:S(2)}) %collective-permute-start.2) | collective-permute-done | bytes 262176 | tf_op jit(solution)/shard_map/ppermute | solution.py:53
  574.2 36.5 %all_to_all.20 = bf16[32,2,2,8,128]{4,3,2,1,0:T(8,128)(2,1)S(1)} all-to-all(bf16[32,2,2,8,128]{4,3,2,1,0:T(8,128)(2,1)S(1)} %copy.246), channel_id=1, replica_groups=mesh['tile'=16,'pos'=32] {'pos'}, dimensions={0} | all-to-all | bytes 524288 | tf_op jit(solution)/shard_map/all_to_all | solution.py:63
  (402 shorter events, 216.5 us)
Async XLA Ops:
  0.6 36.8 %copy-start = (bf16[16,128,128]{2,1,0:T(8,128)(2,1)S(1)}, bf16[16,128,128]{2,1,0:T(8,128)(2,1)}, u32[]{:S(2)}) copy-start(bf16[16,128,128]{2,1,0:T(8,128)(2,1)} %param.16) | copy-start | bytes 1572868
  5.4 14.7 %all-to-all-start = ((s32[16,2,3]{2,1,0:T(2,128)}), s32[16,2,3]{2,1,0:T(2,128)S(1)}, u32[]{:S(2)}, u32[]{:S(2)}) async-start(s32[16,2,3]{2,1,0:T(2,128)} %copy.239), calls=%async_computation | async-start | bytes 32768 | tf_op jit(solution)/shard_map/all_to_all | solution.py:13
  21.0 47.1 %all-to-all-start.1 = ((f32[32,4,8,128]{3,2,1,0:T(8,128)}), f32[32,4,8,128]{3,2,1,0:T(8,128)S(1)}, u32[]{:S(2)}, u32[]{:S(2)}) async-start(f32[32,4,8,128]{3,2,1,0:T(8,128)} %broadcast_in_dim.74), calls=%async_computation.1 | async-start | bytes 1048576 | tf_op jit(solution)/shard_map/all_to_all | solution.py:32
  68.2 22.9 %all-to-all-start.2 = ((bf16[16,2,128,128]{3,2,1,0:T(8,128)(2,1)}), bf16[16,2,128,128]{3,2,1,0:T(8,128)(2,1)}, u32[]{:S(2)}, u32[]{:S(2)}) async-start(bf16[16,2,128,128]{3,2,1,0:T(8,128)(2,1)} %broadcast_select_fusion), calls=%async_computation.2 | async-start | bytes 2097152 | tf_op jit(solution)/shard_map/all_to_all | solution.py:179
  74.9 13.6 %collective-permute-start = (bf16[2,256,128]{2,1,0:T(8,128)(2,1)S(1)}, bf16[2,256,128]{2,1,0:T(8,128)(2,1)S(1)}, u32[]{:S(2)}, u32[]{:S(2)}) collective-permute-start(bf16[2,256,128]{2,1,0:T(8,128)(2,1)S(1)} %get-tuple-element.767), channel_id=1, source_target_pairs={{32,0},{64,32},{96,64},{128,96},{160,128},{192,160},{224,192},{256... | collective-permute-start | bytes 393224 | tf_op jit(solution)/shard_map/ppermute | solution.py:53
  79.8 10.1 %collective-permute-start.1 = (bf16[2,256,128]{2,1,0:T(8,128)(2,1)S(1)}, bf16[2,256,128]{2,1,0:T(8,128)(2,1)S(1)}, u32[]{:S(2)}, u32[]{:S(2)}) collective-permute-start(bf16[2,256,128]{2,1,0:T(8,128)(2,1)S(1)} %get-tuple-element.768), channel_id=1, source_target_pairs={{32,0},{64,32},{96,64},{128,96},{160,128},{192,160},{224,192},{256... | collective-permute-start | bytes 393224 | tf_op jit(solution)/shard_map/ppermute | solution.py:53
  89.9 2.2 copy-start.1
  89.9 2.2 copy-start.2
  557.6 15.4 %collective-permute-start.2 = (bf16[2,2,256,128]{3,2,1,0:T(8,128)(2,1)S(1)}, bf16[2,2,256,128]{3,2,1,0:T(8,128)(2,1)S(1)}, u32[]{:S(2)}, u32[]{:S(2)}) collective-permute-start(bf16[2,2,256,128]{3,2,1,0:T(8,128)(2,1)S(1)} %slice.154), channel_id=1, source_target_pairs={{0,32},{32,64},{64,96},{96,128},{128,160},{160,192},{192,224},{224... | collective-permute-start | bytes 786440 | tf_op jit(solution)/shard_map/ppermute | solution.py:53
where the time goes:
time: 622 us; the launch traced here: 611 us
  local copies, waits for them, and re-layouts  258 us (41%)
  loops' own time  121 us (19%)
  matrix products  54.4 us (9%)
  waiting for transfers between devices  49.9 us (8%)
  other arithmetic  46.9 us (8%)
  starting transfers between devices  43.3 us (7%)
  blocking collectives  36.5 us (6%)
    another operation x4, loops' own time, run_group(): return lax.fori_loop(0, group_len, add_window, running)  120 us
    dynamic_update_slice x32, local copies, waits for them, and re-layouts, add_window(): return lax.dynamic_update_slice(summed, current + slot_terms[k], start)  116 us
    gather x96, local copies, waits for them, and re-layouts  95.2 us
    dynamic_slice x64, local copies, waits for them, and re-layouts, add_window(): start = (anchor, anchor, rows_here[k], cols_here[k])  38.5 us
    add x32, other arithmetic, add_window(): return lax.dynamic_update_slice(summed, current + slot_terms[k], start)  38.1 us
    all_to_all x1, blocking collectives, sent_and_summed(): lax.all_to_all(split_up(shard, dim, length), axis, 0, 0, tiled=True)  36.5 us
    dot_general x64, matrix products, product(): return jnp.einsum('njk,kl->njl', x, a, preferred_element_type=jnp.float32)  29.1 us
    all_to_all x1, waiting for transfers between devices, sent_to_all(): lax.all_to_all(jnp.broadcast_to(shard[None], (length, *shard.shape)), axi...  28.7 us
  transfers between devices with their start and end apart: 6, of which 5 were waited for; matrix products, arithmetic and copies ran while one was open for 1% of the time, Pallas kernels for 0%

commit v1 on v0

v1 whole, which is shorter than its diff:
```python
import functools
import math

import jax
import jax.numpy as jnp
import ml_dtypes
import numpy as np
from jax import lax
from jax.experimental import pallas as pl
from jax.experimental.pallas import tpu as pltpu
from jax.sharding import PartitionSpec as P

BATCH = 4
META_ROWS = 16


def host_tables(edge_len):
    indices = np.arange(edge_len)
    phases = (indices[:, None] * indices[None, :] % edge_len) * (2.0 * math.pi / edge_len)
    wave = np.exp(1j * phases) / math.sqrt(edge_len)
    centred = np.where(indices < edge_len // 2, indices, indices - edge_len)
    kern = np.exp(-0.5j * math.pi * centred * centred / edge_len)
    fresnel = (wave * kern[None, :]) @ wave.conj().T
    fresnel = 0.5 * (fresnel + fresnel.T)

    def rounded(x):
        return x.astype(np.float32).astype(ml_dtypes.bfloat16)

    def left(re, im):
        return np.block([[re, -im], [im, re]])

    def right(re, im):
        return np.block([[re, im], [-im, re]])

    fr, fi = rounded(fresnel.real), rounded(fresnel.imag)
    dr, di = rounded(wave.real), rounded(-wave.imag)
    return np.stack([left(fr, fi), right(fr, fi), left(dr, di), right(dr, di)])


def shifted(value, axis, steps):
    count = lax.axis_size(axis)
    first, last = (max(0, -steps), min(count, count - steps))
    return lax.ppermute(value, axis, [(source, source + steps) for source in range(first, last)])


def pack_kernel(slots, counts, coords, patterns, out, meta, sem, meta_sem, *, n_tile, cap, tile_width, row_max):
    rows = patterns.shape[1]

    def copy(i):
        return pltpu.make_async_copy(
            patterns.at[slots[i]], out.at[i // cap, pl.ds((i % cap) * rows, rows)], sem
        )

    for i in range(n_tile * cap):
        copy(i).start()
    lane = lax.broadcasted_iota(jnp.int32, (META_ROWS, 128), 1)
    for d in range(n_tile):
        value = jnp.zeros((META_ROWS, 128), jnp.int32)
        for c in range(cap):
            j = slots[d * cap + c]
            row = jnp.clip(coords[2 * j], 0, row_max)
            col = jnp.clip(coords[2 * j + 1] - d * tile_width, 0, tile_width)
            live = (c < counts[d]).astype(jnp.int32)
            for k, part in enumerate((row, col, live)):
                value = jnp.where(lane == 3 * c + k, part, value)
        meta[d] = value.astype(jnp.float32).astype(jnp.bfloat16)
    tail = pltpu.make_async_copy(meta, out.at[:, pl.ds(cap * rows, META_ROWS)], meta_sem)
    tail.start()
    for i in range(n_tile * cap):
        copy(i).wait()
    tail.wait()


def pack(patterns, coords, send_slots, send_counts, n_tile, cap, tile_width, row_max):
    rows = patterns.shape[1]
    body = functools.partial(
        pack_kernel, n_tile=n_tile, cap=cap, tile_width=tile_width, row_max=row_max
    )
    return pl.pallas_call(
        body,
        out_shape=jax.ShapeDtypeStruct((n_tile, cap * rows + META_ROWS, 128), jnp.bfloat16),
        in_specs=[
            pl.BlockSpec(memory_space=pltpu.SMEM),
            pl.BlockSpec(memory_space=pltpu.SMEM),
            pl.BlockSpec(memory_space=pltpu.SMEM),
            pl.BlockSpec(memory_space=pl.ANY),
        ],
        out_specs=pl.BlockSpec(memory_space=pl.ANY),
        scratch_shapes=[
            pltpu.VMEM((n_tile, META_ROWS, 128), jnp.bfloat16),
            pltpu.SemaphoreType.DMA,
            pltpu.SemaphoreType.DMA,
        ],
        name="pack",
    )(send_slots, send_counts, coords, patterns)


def grad_kernel(meta, payload, obj, tables, probe, out, slab, acc, order, *, n_tile, cap, n_pos):
    edge = probe.shape[1]
    bf16, f32 = jnp.bfloat16, jnp.float32
    strip = obj.shape[1] // 4
    slot_count = n_tile * cap

    for i in range(slot_count + BATCH):
        order[i] = 0

    def note(i, n):
        live = meta[i // cap, (i % cap) * 3 + 2]

        @pl.when(live > 0)
        def _():
            order[n] = i

        return n + live

    n_live = lax.fori_loop(0, slot_count, note, jnp.int32(0))

    def unpack(p, carry):
        block = obj[p].astype(f32)
        for a in range(4):
            for h in range(2):
                slab[a, h, pl.ds(pl.multiple_of(p * strip, 8), strip), :] = block[
                    a * strip : (a + 1) * strip, h * edge : (h + 1) * edge
                ]
        return carry

    lax.fori_loop(0, n_pos, unpack, 0)
    acc[...] = jnp.zeros(acc.shape, f32)

    lane = lax.broadcasted_iota(jnp.int32, (edge, edge), 1)
    dot = functools.partial(jnp.dot, preferred_element_type=f32)

    def transform(fields, left, right):
        mat_left, mat_right = tables[left], tables[right]
        halves = []
        for k in range(0, len(fields), 2):
            data = jnp.concatenate(
                [jnp.concatenate(pair, axis=0) for pair in fields[k : k + 2]], axis=1
            )
            half = dot(mat_left, data).astype(bf16)
            for h in range(2):
                part = half[:, h * edge : (h + 1) * edge]
                halves.append(jnp.concatenate([part[:edge], part[edge:]], axis=1))
        done = []
        for half in halves:
            full = dot(half, mat_right)
            done.append((full[:, :edge], full[:, edge:]))
        return done

    def times(a, b):
        return (a[0] * b[0] - a[1] * b[1], a[0] * b[1] + a[1] * b[0])

    def conj_times(a, b):
        return (a[0] * b[0] + a[1] * b[1], a[0] * b[1] - a[1] * b[0])

    def rounded(z):
        return (z[0].astype(bf16), z[1].astype(bf16))

    def run_batch(i, carry):
        picks = []
        for b in range(BATCH):
            at = i * BATCH + b
            s = order[at]
            src, c = s // cap, s % cap
            row = meta[src, c * 3]
            col = meta[src, c * 3 + 1]
            weight = (at < n_live).astype(f32)
            picks.append((src, c, row, col, weight, lane >= col))

        def window(b, s):
            _, _, row, _, _, mask = picks[b]
            return tuple(
                jnp.where(
                    mask,
                    slab[part * 2 + s, 0, pl.ds(row, edge), :],
                    slab[part * 2 + s, 1, pl.ds(row, edge), :],
                )
                for part in range(2)
            )

        def rolled_probe(b):
            shift = lax.rem(picks[b][3], edge)
            return (pltpu.roll(probe[0], shift, 1), pltpu.roll(probe[1], shift, 1))

        def add_term(b, s, term):
            _, _, row, _, _, mask = picks[b]
            for part in range(2):
                for h in range(2):
                    piece = jnp.where(mask if h == 0 else ~mask, term[part], 0.0)
                    acc[part * 2 + s, h, pl.ds(row, edge), :] += piece

        exits = [rounded(times(rolled_probe(b), window(b, 0))) for b in range(BATCH)]
        waves = transform(exits, 0, 1)
        exits = [rounded(times(waves[b], window(b, 1))) for b in range(BATCH)]
        far = transform(exits, 2, 3)
        chi = []
        for b in range(BATCH):
            src, c, _, _, weight, _ = picks[b]
            re, im = far[b]
            start = pl.multiple_of(c * edge, edge)
            measured = payload[src, pl.ds(start, edge), :].astype(f32)
            excess = weight * (re * re + im * im - measured)
            chi.append(rounded((excess * re, excess * im)))
        back = transform(chi, 3, 2)
        carried = []
        for b in range(BATCH):
            add_term(b, 1, conj_times(waves[b], back[b]))
            carried.append(rounded(conj_times(window(b, 1), back[b])))
        back = transform(carried, 1, 0)
        for b in range(BATCH):
            add_term(b, 0, conj_times(rolled_probe(b), back[b]))
        return carry

    lax.fori_loop(0, (n_live + BATCH - 1) // BATCH, run_batch, 0)

    def emit(p, carry):
        for a in range(4):
            for h in range(2):
                out[p, a * strip : (a + 1) * strip, h * edge : (h + 1) * edge] = acc[
                    a, h, pl.ds(pl.multiple_of(p * strip, 8), strip), :
                ].astype(bf16)
        return carry

    lax.fori_loop(0, n_pos, emit, 0)


def local_gradient(meta, payload, obj, tables, probe, n_tile, cap, n_pos):
    edge = probe.shape[1]
    rows = n_pos * obj.shape[1] // 4
    body = functools.partial(grad_kernel, n_tile=n_tile, cap=cap, n_pos=n_pos)
    vmem = pl.BlockSpec(memory_space=pltpu.VMEM)
    return pl.pallas_call(
        body,
        out_shape=jax.ShapeDtypeStruct(obj.shape, jnp.bfloat16),
        in_specs=[pl.BlockSpec(memory_space=pltpu.SMEM), vmem, vmem, vmem, vmem],
        out_specs=vmem,
        scratch_shapes=[
            pltpu.VMEM((4, 2, rows, edge), jnp.float32),
            pltpu.VMEM((4, 2, rows, edge), jnp.float32),
            pltpu.SMEM((n_tile * cap + BATCH,), jnp.int32),
        ],
        compiler_params=pltpu.CompilerParams(vmem_limit_bytes=48 * 1024 * 1024),
        name="local_gradient",
    )(meta, payload, obj, tables, probe)


def body(
    patterns, coords, send_slots, send_counts, object_real, object_imag, probe_real, probe_imag
):
    edge_len = probe_real.shape[0]
    slices, strip, tile_width = object_real.shape
    n_tile = lax.axis_size("tile")
    n_pos = lax.axis_size("pos")
    per_source = patterns.shape[0]
    cap = send_slots.shape[2]

    local = jnp.concatenate([object_real, object_imag]).astype(jnp.bfloat16)
    local = local.reshape(2 * slices * strip, tile_width)
    local = jnp.concatenate([local, shifted(local, "tile", -1)], axis=1)
    sent = jnp.broadcast_to(local[None], (n_pos, *local.shape))
    obj = lax.all_to_all(sent, "pos", 0, 0, tiled=True)

    payload = pack(
        patterns,
        coords.reshape(-1),
        send_slots.reshape(-1),
        send_counts.reshape(-1),
        n_tile,
        cap,
        tile_width,
        n_pos * strip - edge_len,
    )
    payload = lax.all_to_all(payload, "tile", 0, 0, tiled=True)
    meta = payload[:, cap * edge_len, :].astype(jnp.int32)

    partial = local_gradient(
        meta,
        payload,
        obj,
        jnp.asarray(host_tables(edge_len)),
        jnp.stack([probe_real, probe_imag]),
        n_tile,
        cap,
        n_pos,
    )
    pieces = lax.all_to_all(partial, "pos", 0, 0, tiled=True)
    share = jnp.sum(pieces.astype(jnp.float32), axis=0)
    share = share * (1.0 / math.sqrt(per_source * n_pos))
    total = share[:, :tile_width] + shifted(share[:, tile_width:], "tile", 1)
    total = total.reshape(2, slices, strip, tile_width)
    return (total[0], total[1])


def solution(mesh):
    in_specs = (
        P(("tile", "pos"), None, None),
        P(("tile", "pos"), None),
        P(("tile", "pos"), None, None),
        P(("tile", "pos"), None),
        P(None, "pos", "tile"),
        P(None, "pos", "tile"),
        P(),
        P(),
    )
    out_specs = (P(None, "pos", "tile"), P(None, "pos", "tile"))
    return jax.shard_map(body, mesh=mesh, in_specs=in_specs, out_specs=out_specs, check_vma=False)
```

time: 622 us -> 171 us (0.27); the launches traced: 611 us -> 168 us
  local copies, waits for them, and re-layouts: 258 us -> 4.22 us
  loops' own time: 121 us -> 0 us
  matrix products: 54.4 us -> 0 us
  other arithmetic: 46.9 us -> 0.13 us
  Pallas kernels: 0 us -> 42.6 us
  starting transfers between devices: 43.3 us -> 30 us
    another operation x9 -> x0, loops' own time: 121 us -> none  [the longest x4 120 us: run_group(): return lax.fori_loop(0, group_len, add_window, running)]
    dynamic_update_slice x32 -> x0, local copies, waits for them, and re-layouts: 116 us -> none  [add_window(): return lax.dynamic_update_slice(summed, current + slot_terms[k], start)]
    gather x99 -> x0, local copies, waits for them, and re-layouts: 96.8 us -> none
    dot_general x132 -> x0, matrix products: 54.4 us -> none  [the longest x64 29.1 us: product(): return jnp.einsum('njk,kl->njl', x, a, preferred_element_type=jnp.float32)]
    pallas_call x0 -> x2, Pallas kernels: none -> 42.6 us  [the longest x1 33.6 us: pack(): pl.pallas_call(body, out_shape=jax.ShapeDtypeStruct((n_tile, cap * rows +...]
    dynamic_slice x68 -> x0, local copies, waits for them, and re-layouts: 38.8 us -> none  [the longest x64 38.5 us: add_window(): start = (anchor, anchor, rows_here[k], cols_here[k])]
    add x32 -> x1, other arithmetic: 38.1 us -> 0.01 us  [body(): total = share[:, :tile_width] + shifted(share[:, tile_width:], 'tile', 1)]
    ppermute x3 -> x2, starting transfers between devices: 14 us -> 6.96 us  [shifted(): lax.ppermute(value, axis, [(source, source + steps) for source in range(f...]
  transfers between devices with their start and end apart: 6 -> 4, of which waited for: 5 -> 4; matrix products, arithmetic and copies ran while one was open for 1% -> 0% of each run, Pallas kernels for 0% -> 0%
where the time goes in v1:
time: 171 us; the launch traced here: 168 us
  waiting for transfers between devices  49.6 us (29%)
  Pallas kernels  42.6 us (25%)
  blocking collectives  40.5 us (24%)
  starting transfers between devices  30 us (18%)
  local copies, waits for them, and re-layouts  4.22 us (2%)
    all_to_all x1, blocking collectives, body(): pieces = lax.all_to_all(partial, 'pos', 0, 0, tiled=True)  40.5 us
    pallas_call x1, Pallas kernels, pack(): pl.pallas_call(body, out_shape=jax.ShapeDtypeStruct((n_tile, cap * rows +...  33.6 us
    all_to_all x1, waiting for transfers between devices, body(): obj = lax.all_to_all(sent, 'pos', 0, 0, tiled=True)  32.8 us
    ppermute x2, waiting for transfers between devices, shifted(): lax.ppermute(value, axis, [(source, source + steps) for source in range(f...  13.9 us
    all_to_all x1, starting transfers between devices, body(): obj = lax.all_to_all(sent, 'pos', 0, 0, tiled=True)  13.6 us
    all_to_all x1, starting transfers between devices, body(): payload = lax.all_to_all(payload, 'tile', 0, 0, tiled=True)  9.42 us
    pallas_call x1, Pallas kernels, local_gradient(): pl.pallas_call(body, out_shape=jax.ShapeDtypeStruct(obj.shape, jnp.bfloat...  9 us
    ppermute x2, starting transfers between devices, shifted(): lax.ppermute(value, axis, [(source, source + steps) for source in range(f...  6.96 us
  transfers between devices with their start and end apart: 4, of which 4 were waited for; matrix products, arithmetic and copies ran while one was open for 0% of the time, Pallas kernels for 0%

profile of v1, /device:TPU:6, one launch (start us, length us, event | category | flops | bytes accessed | tf_op | source)
XLA Modules:
  0.0 167.8 jit_solution(11688719689420371846)
XLA Ops:
  0.6 0.8 copy.13
  1.4 0.6 reshape.24.slots
  2.0 0.8 copy.14
  2.7 0.6 reshape.26.coords
  3.3 33.6 %pack.1 = bf16[16,272,128]{2,1,0:T(8,128)(2,1)} custom-call(s32[32]{0:T(128)} %reshape.24.slots, s32[16]{0:T(128)} %bitcast.13, s32[32]{0:T(128)} %reshape.26.coords, bf16[16,128,128]{2,1,0:T(8,128)(2,1)} %patterns.1), custom_call_target="tpu_custom_call" | custom-call | tf_op jit(solution)/shard_map/pack/pallas_call | solution.py:79
  36.9 0.0 copy-start.3
  36.9 0.0 copy-start.4
  36.9 9.4 %all-to-all-start = ((bf16[16,272,128]{2,1,0:T(8,128)(2,1)}), bf16[16,272,128]{2,1,0:T(8,128)(2,1)S(1)}, u32[]{:S(2)}, u32[]{:S(2)}) async-start(bf16[16,272,128]{2,1,0:T(8,128)(2,1)} %pack.1), calls=%async_computation | async-start | bytes 2228224 | tf_op jit(solution)/shard_map/all_to_all | solution.py:273
  46.4 0.0 copy-done.3
  46.4 0.0 copy-start.1
  46.4 0.0 copy-start.2
  46.4 0.0 copy-start
  46.4 0.0 copy-done.4
  46.5 5.0 %collective-permute-start = (bf16[32,128]{1,0:T(8,128)(2,1)S(1)}, bf16[32,128]{1,0:T(8,128)(2,1)S(1)}, u32[]{:S(2)}, u32[]{:S(2)}) collective-permute-start(bf16[32,128]{1,0:T(8,128)(2,1)S(1)} %maximum_bitcast_fusion), channel_id=1, source_target_pairs={{32,0},{64,32},{96,64},{128,96},{160,128},{192,160},{224,192},{256... | collective-permute-start | bytes 24584 | tf_op jit(solution)/shard_map/ppermute | solution.py:43
  51.5 8.3 %collective-permute-done = bf16[32,128]{1,0:T(8,128)(2,1)S(1)} collective-permute-done((bf16[32,128]{1,0:T(8,128)(2,1)S(1)}, bf16[32,128]{1,0:T(8,128)(2,1)S(1)}, u32[]{:S(2)}, u32[]{:S(2)}) %collective-permute-start) | collective-permute-done | bytes 8224 | tf_op jit(solution)/shard_map/ppermute | solution.py:43
  59.8 3.0 %all-to-all-done.payload = bf16[16,272,128]{2,1,0:T(8,128)(2,1)S(1)} async-done(((bf16[16,272,128]{2,1,0:T(8,128)(2,1)}), bf16[16,272,128]{2,1,0:T(8,128)(2,1)S(1)}, u32[]{:S(2)}, u32[]{:S(2)}) %all-to-all-start) | async-done | bytes 1114144 | tf_op jit(solution)/shard_map/all_to_all | solution.py:273
  62.8 0.9 broadcast_in_dim.2
  63.7 13.6 %all-to-all-start.1 = ((bf16[32,32,256]{2,1,0:T(8,128)(2,1)}), bf16[32,32,256]{2,1,0:T(8,128)(2,1)S(1)}, u32[]{:S(2)}, u32[]{:S(2)}) async-start(bf16[32,32,256]{2,1,0:T(8,128)(2,1)} %broadcast_in_dim.2), calls=%async_computation.1 | async-start | bytes 1048576 | tf_op jit(solution)/shard_map/all_to_all | solution.py:261
  77.3 0.0 copy-done.1
  77.3 0.0 copy-done.2
  77.4 32.8 %all-to-all-done.1.obj = bf16[32,32,256]{2,1,0:T(8,128)(2,1)S(1)} async-done(((bf16[32,32,256]{2,1,0:T(8,128)(2,1)}), bf16[32,32,256]{2,1,0:T(8,128)(2,1)S(1)}, u32[]{:S(2)}, u32[]{:S(2)}) %all-to-all-start.1) | async-done | bytes 524320 | tf_op jit(solution)/shard_map/all_to_all | solution.py:261
  110.2 0.0 copy-done
  110.2 9.0 %local_gradient.1 = bf16[32,32,256]{2,1,0:T(8,128)(2,1)S(1)} custom-call(s32[16,128]{1,0:T(8,128)S(1)} %bitcast.10, bf16[16,272,128]{2,1,0:T(8,128)(2,1)S(1)} %all-to-all-done.payload, bf16[32,32,256]{2,1,0:T(8,128)(2,1)S(1)} %all-to-all-done.1.obj, bf16[4,256,256]{2,1,0:T(8,128)(2,1)S(1)} %copy-done, f32[2,128,128]{2,1,0:T(8,128)S(1)} %pad_maximum_fusion.probe), custom_call_target="tpu_custom_call" | custom-call | tf_op jit(solution)/shard_map/local_gradient/pallas_call | solution.py:232
  119.2 40.5 %all_to_all.15 = bf16[32,32,256]{2,1,0:T(8,128)(2,1)S(1)} all-to-all(bf16[32,32,256]{2,1,0:T(8,128)(2,1)S(1)} %local_gradient.1), channel_id=1, replica_groups=mesh['tile'=16,'pos'=32] {'pos'}, dimensions={0} | all-to-all | bytes 1048576 | tf_op jit(solution)/shard_map/all_to_all | solution.py:286
  159.6 0.1 convert_reduce_fusion
  159.7 1.9 %collective-permute-start.1 = (f32[32,128]{1,0:T(8,128)S(1)}, f32[32,128]{1,0:T(8,128)S(1)}, u32[]{:S(2)}, u32[]{:S(2)}) collective-permute-start(f32[32,128]{1,0:T(8,128)S(1)} %slice.24), channel_id=1, source_target_pairs={{0,32},{32,64},{64,96},{96,128},{128,160},{160,192},{192,224},{224... | collective-permute-start | bytes 49160 | tf_op jit(solution)/shard_map/ppermute | solution.py:43
  161.7 5.5 %collective-permute-done.1 = f32[32,128]{1,0:T(8,128)S(1)} collective-permute-done((f32[32,128]{1,0:T(8,128)S(1)}, f32[32,128]{1,0:T(8,128)S(1)}, u32[]{:S(2)}, u32[]{:S(2)}) %collective-permute-start.1) | collective-permute-done | bytes 16416 | tf_op jit(solution)/shard_map/ppermute | solution.py:43
  167.2 0.6 slice_bitcast_fusion
  (9 shorter events, 0.1 us)
Async XLA Ops:
  36.9 9.5 %copy-start.3 = (f32[2,8,128]{2,1,0:T(8,128)S(1)}, f32[2,8,128]{2,1,0:T(8,128)}, u32[]{:S(2)}) copy-start(f32[2,8,128]{2,1,0:T(8,128)} %param.14) | copy-start | bytes 24580
  36.9 9.5 %copy-start.4 = (f32[2,8,128]{2,1,0:T(8,128)S(1)}, f32[2,8,128]{2,1,0:T(8,128)}, u32[]{:S(2)}) copy-start(f32[2,8,128]{2,1,0:T(8,128)} %param.13) | copy-start | bytes 24580
  36.9 25.9 %all-to-all-start = ((bf16[16,272,128]{2,1,0:T(8,128)(2,1)}), bf16[16,272,128]{2,1,0:T(8,128)(2,1)S(1)}, u32[]{:S(2)}, u32[]{:S(2)}) async-start(bf16[16,272,128]{2,1,0:T(8,128)(2,1)} %pack.1), calls=%async_computation | async-start | bytes 2228224 | tf_op jit(solution)/shard_map/all_to_all | solution.py:273
  46.4 31.0 %copy-start.1 = (f32[128,128]{1,0:T(8,128)S(1)}, f32[128,128]{1,0:T(8,128)}, u32[]{:S(2)}) copy-start(f32[128,128]{1,0:T(8,128)} %param.16) | copy-start | bytes 196612
  46.4 31.0 %copy-start.2 = (f32[128,128]{1,0:T(8,128)S(1)}, f32[128,128]{1,0:T(8,128)}, u32[]{:S(2)}) copy-start(f32[128,128]{1,0:T(8,128)} %param.15) | copy-start | bytes 196612
  46.4 63.8 %copy-start = (bf16[4,256,256]{2,1,0:T(8,128)(2,1)S(1)}, bf16[4,256,256]{2,1,0:T(8,128)(2,1)}, u32[]{:S(2)}) copy-start(bf16[4,256,256]{2,1,0:T(8,128)(2,1)} %constant.6.clone.tables) | copy-start | bytes 1572868
  46.5 13.4 %collective-permute-start = (bf16[32,128]{1,0:T(8,128)(2,1)S(1)}, bf16[32,128]{1,0:T(8,128)(2,1)S(1)}, u32[]{:S(2)}, u32[]{:S(2)}) collective-permute-start(bf16[32,128]{1,0:T(8,128)(2,1)S(1)} %maximum_bitcast_fusion), channel_id=1, source_target_pairs={{32,0},{64,32},{96,64},{128,96},{160,128},{192,160},{224,192},{256... | collective-permute-start | bytes 24584 | tf_op jit(solution)/shard_map/ppermute | solution.py:43
  63.7 46.5 %all-to-all-start.1 = ((bf16[32,32,256]{2,1,0:T(8,128)(2,1)}), bf16[32,32,256]{2,1,0:T(8,128)(2,1)S(1)}, u32[]{:S(2)}, u32[]{:S(2)}) async-start(bf16[32,32,256]{2,1,0:T(8,128)(2,1)} %broadcast_in_dim.2), calls=%async_computation.1 | async-start | bytes 1048576 | tf_op jit(solution)/shard_map/all_to_all | solution.py:261
  159.7 7.5 %collective-permute-start.1 = (f32[32,128]{1,0:T(8,128)S(1)}, f32[32,128]{1,0:T(8,128)S(1)}, u32[]{:S(2)}, u32[]{:S(2)}) collective-permute-start(f32[32,128]{1,0:T(8,128)S(1)} %slice.24), channel_id=1, source_target_pairs={{0,32},{32,64},{64,96},{96,128},{128,160},{160,192},{192,224},{224... | collective-permute-start | bytes 49160 | tf_op jit(solution)/shard_map/ppermute | solution.py:43

commit v2 on v1

v2 whole, which is shorter than its diff:
```python
import functools
import math

import jax
import jax.numpy as jnp
import ml_dtypes
import numpy as np
from jax import lax
from jax.experimental import pallas as pl
from jax.experimental.pallas import tpu as pltpu
from jax.sharding import PartitionSpec as P

BATCH = 16
CHUNK = 16
META_ROWS = 16


def host_tables(edge_len):
    indices = np.arange(edge_len)
    phases = (indices[:, None] * indices[None, :] % edge_len) * (2.0 * math.pi / edge_len)
    wave = np.exp(1j * phases) / math.sqrt(edge_len)
    centred = np.where(indices < edge_len // 2, indices, indices - edge_len)
    kern = np.exp(-0.5j * math.pi * centred * centred / edge_len)
    fresnel = (wave * kern[None, :]) @ wave.conj().T
    fresnel = 0.5 * (fresnel + fresnel.T)

    def rounded(x):
        return x.astype(np.float32).astype(ml_dtypes.bfloat16)

    def left(re, im):
        return np.block([[re, -im], [im, re]])

    def right(re, im):
        return np.block([[re, im], [-im, re]])

    fr, fi = rounded(fresnel.real), rounded(fresnel.imag)
    dr, di = rounded(wave.real), rounded(-wave.imag)
    return np.stack([left(fr, fi), right(fr, fi), left(dr, di), right(dr, di)])


def pack_kernel(slots, counts, coords, patterns, out, *, n_tile, cap, tile_width, row_max):
    rows = patterns.shape[1]
    lane = lax.broadcasted_iota(jnp.int32, (META_ROWS, 128), 1)
    for d in range(n_tile):
        value = jnp.zeros((META_ROWS, 128), jnp.int32)
        for c in range(cap):
            j = slots[c, d]
            out[d, c * rows : (c + 1) * rows, :] = patterns[j]
            row = jnp.clip(coords[0, j], 0, row_max)
            col = jnp.clip(coords[1, j] - d * tile_width, 0, tile_width)
            live = (c < counts[0, d]).astype(jnp.int32)
            for k, part in enumerate((row, col, live)):
                value = jnp.where(lane == 3 * c + k, part, value)
        out[d, cap * rows :, :] = value.astype(jnp.float32).astype(jnp.bfloat16)


def pack(patterns, coords, send_slots, send_counts, cap, tile_width, row_max):
    rows = patterns.shape[1]
    n_tile = send_counts.shape[1]
    body = functools.partial(
        pack_kernel, n_tile=n_tile, cap=cap, tile_width=tile_width, row_max=row_max
    )
    smem = pl.BlockSpec(memory_space=pltpu.SMEM)
    vmem = pl.BlockSpec(memory_space=pltpu.VMEM)
    return pl.pallas_call(
        body,
        out_shape=jax.ShapeDtypeStruct((n_tile, cap * rows + META_ROWS, 128), jnp.bfloat16),
        in_specs=[smem, smem, smem, vmem],
        out_specs=vmem,
        name="pack",
    )(send_slots, send_counts, coords, patterns)


def grad_kernel(
    here,
    meta,
    payload,
    mine,
    mine_next,
    other,
    other_next,
    tables,
    probe,
    own_out,
    spill_out,
    slab,
    acc,
    order,
    data,
    half,
    field,
    wave,
    rolled,
    *,
    cap,
):
    edge = probe.shape[1]
    bf16, f32 = jnp.bfloat16, jnp.float32
    strip = mine.shape[1] // 4
    slot_count = meta.shape[0] * cap

    for i in range(slot_count + BATCH):
        order[i] = 0

    def note(i, n):
        live = meta[i // cap, (i % cap) * 3 + 2]

        @pl.when(live > 0)
        def _():
            order[n] = i

        return n + live

    n_live = lax.fori_loop(0, slot_count, note, jnp.int32(0))

    def unpack(z, carry):
        for ref, y, h in (
            (mine, here[0], 0),
            (mine_next, here[0], 1),
            (other, 1 - here[0], 0),
            (other_next, 1 - here[0], 1),
        ):
            block = ref[z].astype(f32)
            at = pl.multiple_of((2 * z + y) * strip, 8)
            for a in range(4):
                slab[a, h, pl.ds(at, strip), :] = block[a * strip : (a + 1) * strip]
        return carry

    lax.fori_loop(0, mine.shape[0], unpack, 0, unroll=4)
    acc[...] = jnp.zeros(acc.shape, f32)

    lane = lax.broadcasted_iota(jnp.int32, (CHUNK, edge), 1)
    dot = functools.partial(jnp.dot, preferred_element_type=f32)
    chunks = range(0, edge, CHUNK)

    def transform(left, right):
        for b in range(0, BATCH, 2):
            full = dot(tables[left], data[:, b * edge : (b + 2) * edge]).astype(bf16)
            for h in range(2):
                for k in range(2):
                    half[(b + h) * edge : (b + h + 1) * edge, k * edge : (k + 1) * edge] = full[
                        k * edge : (k + 1) * edge, h * edge : (h + 1) * edge
                    ]

    def finish(right, target):
        for b in range(0, BATCH, 2):
            target[b * edge : (b + 2) * edge, :] = dot(half[b * edge : (b + 2) * edge, :], tables[right])

    def times(a, b):
        return (a[0] * b[0] - a[1] * b[1], a[0] * b[1] + a[1] * b[0])

    def conj_times(a, b):
        return (a[0] * b[0] + a[1] * b[1], a[0] * b[1] - a[1] * b[0])

    def keep(b, r, z):
        for k in range(2):
            data[k * edge + r : k * edge + r + CHUNK, b * edge : (b + 1) * edge] = z[k].astype(bf16)

    def read(ref, b, r):
        at = b * edge + r
        return (ref[at : at + CHUNK, :edge], ref[at : at + CHUNK, edge:])

    def run_batch(i, carry):
        picks = []
        for b in range(BATCH):
            at = i * BATCH + b
            s = order[at]
            src, c = s // cap, s % cap
            row = meta[src, c * 3]
            col = meta[src, c * 3 + 1]
            weight = (at < n_live).astype(f32)
            picks.append((src, c, row, col, weight, lane >= col))

        def window(b, s, r):
            _, _, row, _, _, mask = picks[b]
            return tuple(
                jnp.where(
                    mask,
                    slab[part * 2 + s, 0, pl.ds(row + r, CHUNK), :],
                    slab[part * 2 + s, 1, pl.ds(row + r, CHUNK), :],
                )
                for part in range(2)
            )

        def add_term(b, s, r, term):
            _, _, row, _, _, mask = picks[b]
            for part in range(2):
                for h in range(2):
                    piece = jnp.where(mask, term[part], 0.0) if h == 0 else jnp.where(mask, 0.0, term[part])
                    acc[part * 2 + s, h, pl.ds(row + r, CHUNK), :] += piece

        for b in range(BATCH):
            shift = lax.rem(picks[b][3], edge)
            for r in chunks:
                at = b * edge + r
                re = pltpu.roll(probe[0, r : r + CHUNK, :], shift, 1)
                im = pltpu.roll(probe[1, r : r + CHUNK, :], shift, 1)
                rolled[at : at + CHUNK, :edge] = re
                rolled[at : at + CHUNK, edge:] = im
                keep(b, r, times((re, im), window(b, 0, r)))
        transform(0, 1)
        finish(1, wave)
        for b in range(BATCH):
            for r in chunks:
                keep(b, r, times(read(wave, b, r), window(b, 1, r)))
        transform(2, 3)
        finish(3, field)
        for b in range(BATCH):
            src, c, _, _, weight, _ = picks[b]
            for r in chunks:
                re, im = read(field, b, r)
                start = pl.multiple_of(c * edge + r, CHUNK)
                measured = payload[src, pl.ds(start, CHUNK), :].astype(f32)
                excess = weight * (re * re + im * im - measured)
                keep(b, r, (excess * re, excess * im))
        transform(3, 2)
        finish(2, field)
        for b in range(BATCH):
            for r in chunks:
                back = read(field, b, r)
                add_term(b, 1, r, conj_times(read(wave, b, r), back))
                keep(b, r, conj_times(window(b, 1, r), back))
        transform(1, 0)
        finish(0, field)
        for b in range(BATCH):
            for r in chunks:
                add_term(b, 0, r, conj_times(read(rolled, b, r), read(field, b, r)))
        return carry

    lax.fori_loop(0, (n_live + BATCH - 1) // BATCH, run_batch, 0)

    def emit(p, carry):
        at = pl.multiple_of(p * strip, 8)
        for a in range(4):
            for h, ref in enumerate((own_out, spill_out)):
                ref[p, a * strip : (a + 1) * strip, :] = acc[a, h, pl.ds(at, strip), :].astype(bf16)
        return carry

    lax.fori_loop(0, own_out.shape[0], emit, 0, unroll=4)


def local_gradient(here, meta, payload, strips, tables, probe, cap):
    edge = probe.shape[1]
    n_pos = 2 * strips[0].shape[0]
    rows = n_pos * strips[0].shape[1] // 4
    share = jax.ShapeDtypeStruct((n_pos, *strips[0].shape[1:]), jnp.bfloat16)
    smem = pl.BlockSpec(memory_space=pltpu.SMEM)
    vmem = pl.BlockSpec(memory_space=pltpu.VMEM)
    return pl.pallas_call(
        functools.partial(grad_kernel, cap=cap),
        out_shape=(share, share),
        in_specs=[smem, smem, vmem, vmem, vmem, vmem, vmem, vmem, vmem],
        out_specs=(vmem, vmem),
        scratch_shapes=[
            pltpu.VMEM((4, 2, rows, edge), jnp.float32),
            pltpu.VMEM((4, 2, rows, edge), jnp.float32),
            pltpu.SMEM((meta.shape[0] * cap + BATCH,), jnp.int32),
            pltpu.VMEM((2 * edge, BATCH * edge), jnp.bfloat16),
            pltpu.VMEM((BATCH * edge, 2 * edge), jnp.bfloat16),
            pltpu.VMEM((BATCH * edge, 2 * edge), jnp.float32),
            pltpu.VMEM((BATCH * edge, 2 * edge), jnp.float32),
            pltpu.VMEM((BATCH * edge, 2 * edge), jnp.float32),
        ],
        compiler_params=pltpu.CompilerParams(vmem_limit_bytes=48 * 1024 * 1024),
        name="local_gradient",
    )(here, meta, payload, *strips, tables, probe)


def moved(value, tile_step, flip):
    n_tile, n_pos = lax.axis_size("tile"), lax.axis_size("pos")
    pairs = []
    for t in range(n_tile):
        if 0 <= t + tile_step < n_tile:
            for p in range(n_pos):
                source = (t + tile_step) * n_pos + (p ^ 1 if flip else p)
                pairs.append((source, t * n_pos + p))
    return lax.ppermute(value, ("tile", "pos"), pairs)


def body(
    patterns, coords, send_slots, send_counts, object_real, object_imag, probe_real, probe_imag
):
    edge_len = probe_real.shape[0]
    slices, strip, tile_width = object_real.shape
    n_pos = lax.axis_size("pos")
    per_source = patterns.shape[0]
    cap = send_slots.shape[2]

    local = jnp.concatenate([object_real, object_imag]).astype(jnp.bfloat16)
    local = local.reshape(2 * slices * strip, tile_width)
    sent = jnp.broadcast_to(local[None], (n_pos // 2, *local.shape))
    same_y = [[2 * z + y for z in range(n_pos // 2)] for y in range(2)]
    mine = lax.all_to_all(sent, "pos", 0, 0, axis_index_groups=same_y, tiled=True)

    payload = pack(
        patterns,
        coords.T,
        send_slots[0].T,
        send_counts,
        cap,
        tile_width,
        n_pos * strip - edge_len,
    )
    mine, payload = lax.optimization_barrier((mine, payload))
    strips = (mine, moved(mine, 1, False), moved(mine, 0, True), moved(mine, 1, True))
    payload = lax.all_to_all(payload, "tile", 0, 0, tiled=True)
    meta = payload[:, cap * edge_len, :].astype(jnp.int32)

    own, spill = local_gradient(
        (lax.axis_index("pos") % 2).astype(jnp.int32).reshape(1),
        meta,
        payload,
        strips,
        jnp.asarray(host_tables(edge_len)),
        jnp.stack([probe_real, probe_imag]),
        cap,
    )
    total = own.astype(jnp.float32) + moved(spill, -1, False).astype(jnp.float32)
    pieces = lax.all_to_all(total.astype(jnp.bfloat16), "pos", 0, 0, tiled=True)
    share = jnp.sum(pieces.astype(jnp.float32), axis=0)
    share = share * (1.0 / math.sqrt(per_source * n_pos))
    share = share.reshape(2, slices, strip, tile_width)
    return (share[0], share[1])


def solution(mesh):
    in_specs = (
        P(("tile", "pos"), None, None),
        P(("tile", "pos"), None),
        P(("tile", "pos"), None, None),
        P(("tile", "pos"), None),
        P(None, "pos", "tile"),
        P(None, "pos", "tile"),
        P(),
        P(),
    )
    out_specs = (P(None, "pos", "tile"), P(None, "pos", "tile"))
    return jax.shard_map(body, mesh=mesh, in_specs=in_specs, out_specs=out_specs, check_vma=False)
```

time: 171 us -> 107 us (0.63); the launches traced: 168 us -> 106 us
  Pallas kernels: 42.6 us -> 8.63 us
  waiting for transfers between devices: 49.6 us -> 28.3 us
  blocking collectives: 40.5 us -> 31 us
  starting transfers between devices: 30 us -> 34.8 us
  local copies, waits for them, and re-layouts: 4.22 us -> 1.29 us
    pallas_call x1, Pallas kernels: 33.6 us -> 2.26 us  [pack(): pl.pallas_call(body, out_shape=jax.ShapeDtypeStruct((n_tile, cap * rows +...]
    all_to_all x1, waiting for transfers between devices: 32.8 us -> 12.4 us  [body(): lax.all_to_all(sent, 'pos', 0, 0, axis_index_groups=same_y, tiled=True)]
    all_to_all x1, blocking collectives: 40.5 us -> 31 us  [body(): pieces = lax.all_to_all(total.astype(jnp.bfloat16), 'pos', 0, 0, tiled=True)]
    ppermute x2 -> x4, starting transfers between devices: 6.96 us -> 12.2 us  [moved(): return lax.ppermute(value, ('tile', 'pos'), pairs)]
    ppermute x2 -> x4, waiting for transfers between devices: 13.9 us -> 8.82 us  [moved(): return lax.ppermute(value, ('tile', 'pos'), pairs)]
    all_to_all x1, waiting for transfers between devices: 3.01 us -> 7.05 us  [body(): payload = lax.all_to_all(payload, 'tile', 0, 0, tiled=True)]
    pallas_call x1, Pallas kernels: 9 us -> 6.37 us  [local_gradient(): pl.pallas_call(functools.partial(grad_kernel, cap=cap), out_shape=(share,...]
    all_to_all x1, starting transfers between devices: 9.42 us -> 7.43 us  [body(): payload = lax.all_to_all(payload, 'tile', 0, 0, tiled=True)]
  transfers between devices with their start and end apart: 4 -> 6, of which waited for: 4 -> 5; matrix products, arithmetic and copies ran while one was open for 0% -> 0% of each run, Pallas kernels for 0% -> 2%
where the time goes in v2:
time: 107 us; the launch traced here: 106 us
  starting transfers between devices  34.8 us (33%)
  blocking collectives  31 us (29%)
  waiting for transfers between devices  28.3 us (26%)
  Pallas kernels  8.63 us (8%)
  other arithmetic  1.56 us (1%)
  local copies, waits for them, and re-layouts  1.29 us (1%)
    all_to_all x1, blocking collectives, body(): pieces = lax.all_to_all(total.astype(jnp.bfloat16), 'pos', 0, 0, tiled=True)  31 us
    all_to_all x1, starting transfers between devices, body(): lax.all_to_all(sent, 'pos', 0, 0, axis_index_groups=same_y, tiled=True)  15.2 us
    all_to_all x1, waiting for transfers between devices, body(): lax.all_to_all(sent, 'pos', 0, 0, axis_index_groups=same_y, tiled=True)  12.4 us
    ppermute x4, starting transfers between devices, moved(): return lax.ppermute(value, ('tile', 'pos'), pairs)  12.2 us
    ppermute x4, waiting for transfers between devices, moved(): return lax.ppermute(value, ('tile', 'pos'), pairs)  8.82 us
    all_to_all x1, starting transfers between devices, body(): payload = lax.all_to_all(payload, 'tile', 0, 0, tiled=True)  7.43 us
    all_to_all x1, waiting for transfers between devices, body(): payload = lax.all_to_all(payload, 'tile', 0, 0, tiled=True)  7.05 us
    pallas_call x1, Pallas kernels, local_gradient(): pl.pallas_call(functools.partial(grad_kernel, cap=cap), out_shape=(share,...  6.37 us
  transfers between devices with their start and end apart: 6, of which 5 were waited for; matrix products, arithmetic and copies ran while one was open for 0% of the time, Pallas kernels for 2%

profile of v2, /device:TPU:6, one launch (start us, length us, event | category | flops | bytes accessed | tf_op | source)
XLA Modules:
  0.0 106.3 jit_solution(15296369259619186011)
XLA Ops:
  0.6 0.7 convert.8
  1.3 0.7 convert.7
  2.0 0.7 broadcast_in_dim.2
  2.7 15.2 %all-to-all-start = ((bf16[16,32,128]{2,1,0:T(8,128)(2,1)}), bf16[16,32,128]{2,1,0:T(8,128)(2,1)S(1)}, u32[]{:S(2)}, u32[]{:S(2)}) async-start(bf16[16,32,128]{2,1,0:T(8,128)(2,1)} %broadcast_in_dim.2), calls=%async_computation | async-start | bytes 262144 | tf_op jit(solution)/shard_map/all_to_all | solution.py:293
  17.9 2.3 %pack.1 = bf16[16,272,128]{2,1,0:T(8,128)(2,1)} custom-call(s32[2,16]{1,0:T(2,128)} %bitcast.17, s32[1,16]{1,0:T(1,128)} %counts.1, s32[2,16]{1,0:T(2,128)} %bitcast.18, bf16[16,128,128]{2,1,0:T(8,128)(2,1)} %patterns.1), custom_call_target="tpu_custom_call" | custom-call | tf_op jit(solution)/shard_map/pack/pallas_call | solution.py:65
  20.2 0.0 copy-start.1
  20.2 0.0 copy-start.2
  20.2 0.0 copy-start
  20.2 12.4 %all-to-all-done.mine = bf16[16,32,128]{2,1,0:T(8,128)(2,1)S(1)} async-done(((bf16[16,32,128]{2,1,0:T(8,128)(2,1)}), bf16[16,32,128]{2,1,0:T(8,128)(2,1)S(1)}, u32[]{:S(2)}, u32[]{:S(2)}) %all-to-all-start) | async-done | bytes 131104 | tf_op jit(solution)/shard_map/all_to_all | solution.py:293
  32.6 7.4 %all-to-all-start.1 = ((bf16[16,272,128]{2,1,0:T(8,128)(2,1)}), bf16[16,272,128]{2,1,0:T(8,128)(2,1)S(1)}, u32[]{:S(2)}, u32[]{:S(2)}) async-start(bf16[16,272,128]{2,1,0:T(8,128)(2,1)} %pack.1), calls=%async_computation.1 | async-start | bytes 2228224 | tf_op jit(solution)/shard_map/all_to_all | solution.py:306
  40.0 0.0 copy-done.1
  40.0 0.0 copy-done.2
  40.1 4.9 %collective-permute-start = (bf16[16,32,128]{2,1,0:T(8,128)(2,1)S(1)}, bf16[16,32,128]{2,1,0:T(8,128)(2,1)S(1)}, u32[]{:S(2)}, u32[]{:S(2)}) collective-permute-start(bf16[16,32,128]{2,1,0:T(8,128)(2,1)S(1)} %all-to-all-done.mine), channel_id=1, source_target_pairs={{32,0},{33,1},{34,2},{35,3},{36,4},{37,5},{38,6},{39,7},{40,8},{41... | collective-permute-start | bytes 393224 | tf_op jit(solution)/shard_map/ppermute | solution.py:277
  45.0 2.6 %collective-permute-start.1 = (bf16[16,32,128]{2,1,0:T(8,128)(2,1)S(1)}, bf16[16,32,128]{2,1,0:T(8,128)(2,1)S(1)}, u32[]{:S(2)}, u32[]{:S(2)}) collective-permute-start(bf16[16,32,128]{2,1,0:T(8,128)(2,1)S(1)} %all-to-all-done.mine), channel_id=1, source_target_pairs={{1,0},{0,1},{3,2},{2,3},{5,4},{4,5},{7,6},{6,7},{9,8},{8,9},{11,10... | collective-permute-start | bytes 393224 | tf_op jit(solution)/shard_map/ppermute | solution.py:277
  47.6 1.9 %collective-permute-start.2 = (bf16[16,32,128]{2,1,0:T(8,128)(2,1)S(1)}, bf16[16,32,128]{2,1,0:T(8,128)(2,1)S(1)}, u32[]{:S(2)}, u32[]{:S(2)}) collective-permute-start(bf16[16,32,128]{2,1,0:T(8,128)(2,1)S(1)} %all-to-all-done.mine), channel_id=1, source_target_pairs={{33,0},{32,1},{35,2},{34,3},{37,4},{36,5},{39,6},{38,7},{41,8},{40... | collective-permute-start | bytes 393224 | tf_op jit(solution)/shard_map/ppermute | solution.py:277
  49.5 7.1 %all-to-all-done.1.payload = bf16[16,272,128]{2,1,0:T(8,128)(2,1)S(1)} async-done(((bf16[16,272,128]{2,1,0:T(8,128)(2,1)}), bf16[16,272,128]{2,1,0:T(8,128)(2,1)S(1)}, u32[]{:S(2)}, u32[]{:S(2)}) %all-to-all-start.1) | async-done | bytes 1114144 | tf_op jit(solution)/shard_map/all_to_all | solution.py:306
  56.6 0.0 collective-permute-done.mine_next
  56.6 0.5 collective-permute-done.1.other
  57.1 0.9 collective-permute-done.2.other_next
  58.1 0.0 copy-done
  58.1 6.4 %local_gradient.1 = (bf16[32,32,128]{2,1,0:T(8,128)(2,1)S(1)}, bf16[32,32,128]{2,1,0:T(8,128)(2,1)S(1)}) custom-call(s32[1]{0:T(128)} %bitcast.here, s32[16,128]{1,0:T(8,128)S(1)} %bitcast.14, bf16[16,272,128]{2,1,0:T(8,128)(2,1)S(1)} %all-to-all-done.1.payload, bf16[16,32,128]{2,1,0:T(8,128)(2,1)S(1)} %all-to-all-done.mine, ...), custom_call_target="tpu_custom_call" | custom-call | tf_op jit(solution)/shard_map/local_gradient/pallas_call | solution.py:249
  64.4 2.7 %collective-permute-start.3 = (bf16[32,32,128]{2,1,0:T(8,128)(2,1)S(1)}, bf16[32,32,128]{2,1,0:T(8,128)(2,1)S(1)}, u32[]{:S(2)}, u32[]{:S(2)}) collective-permute-start(bf16[32,32,128]{2,1,0:T(8,128)(2,1)S(1)} %get-tuple-element.9), channel_id=1, source_target_pairs={{0,32},{1,33},{2,34},{3,35},{4,36},{5,37},{6,38},{7,39},{8,40},{9,... | collective-permute-start | bytes 786440 | tf_op jit(solution)/shard_map/ppermute | solution.py:277
  67.2 7.3 %collective-permute-done.3 = bf16[32,32,128]{2,1,0:T(8,128)(2,1)S(1)} collective-permute-done((bf16[32,32,128]{2,1,0:T(8,128)(2,1)S(1)}, bf16[32,32,128]{2,1,0:T(8,128)(2,1)S(1)}, u32[]{:S(2)}, u32[]{:S(2)}) %collective-permute-start.3) | collective-permute-done | bytes 262176 | tf_op jit(solution)/shard_map/ppermute | solution.py:277
  74.5 0.1 add_convert_fusion
  74.6 31.0 %all_to_all.15 = bf16[32,32,128]{2,1,0:T(8,128)(2,1)S(1)} all-to-all(bf16[32,32,128]{2,1,0:T(8,128)(2,1)S(1)} %add_convert_fusion), channel_id=1, replica_groups=mesh['tile'=16,'pos'=32] {'pos'}, dimensions={0} | all-to-all | bytes 524288 | tf_op jit(solution)/shard_map/all_to_all | solution.py:319
  105.6 0.6 slice_bitcast_fusion
  (5 shorter events, 0.1 us)
Async XLA Ops:
  2.7 29.9 %all-to-all-start = ((bf16[16,32,128]{2,1,0:T(8,128)(2,1)}), bf16[16,32,128]{2,1,0:T(8,128)(2,1)S(1)}, u32[]{:S(2)}, u32[]{:S(2)}) async-start(bf16[16,32,128]{2,1,0:T(8,128)(2,1)} %broadcast_in_dim.2), calls=%async_computation | async-start | bytes 262144 | tf_op jit(solution)/shard_map/all_to_all | solution.py:293
  20.2 19.9 %copy-start.1 = (f32[128,128]{1,0:T(8,128)S(1)}, f32[128,128]{1,0:T(8,128)}, u32[]{:S(2)}) copy-start(f32[128,128]{1,0:T(8,128)} %param.16) | copy-start | bytes 196612
  20.2 19.9 %copy-start.2 = (f32[128,128]{1,0:T(8,128)S(1)}, f32[128,128]{1,0:T(8,128)}, u32[]{:S(2)}) copy-start(f32[128,128]{1,0:T(8,128)} %param.15) | copy-start | bytes 196612
  20.2 37.9 %copy-start = (bf16[4,256,256]{2,1,0:T(8,128)(2,1)S(1)}, bf16[4,256,256]{2,1,0:T(8,128)(2,1)}, u32[]{:S(2)}) copy-start(bf16[4,256,256]{2,1,0:T(8,128)(2,1)} %constant.23.clone.tables) | copy-start | bytes 1572868
  32.6 24.0 %all-to-all-start.1 = ((bf16[16,272,128]{2,1,0:T(8,128)(2,1)}), bf16[16,272,128]{2,1,0:T(8,128)(2,1)S(1)}, u32[]{:S(2)}, u32[]{:S(2)}) async-start(bf16[16,272,128]{2,1,0:T(8,128)(2,1)} %pack.1), calls=%async_computation.1 | async-start | bytes 2228224 | tf_op jit(solution)/shard_map/all_to_all | solution.py:306
  40.1 16.5 %collective-permute-start = (bf16[16,32,128]{2,1,0:T(8,128)(2,1)S(1)}, bf16[16,32,128]{2,1,0:T(8,128)(2,1)S(1)}, u32[]{:S(2)}, u32[]{:S(2)}) collective-permute-start(bf16[16,32,128]{2,1,0:T(8,128)(2,1)S(1)} %all-to-all-done.mine), channel_id=1, source_target_pairs={{32,0},{33,1},{34,2},{35,3},{36,4},{37,5},{38,6},{39,7},{40,8},{41... | collective-permute-start | bytes 393224 | tf_op jit(solution)/shard_map/ppermute | solution.py:277
  45.0 12.1 %collective-permute-start.1 = (bf16[16,32,128]{2,1,0:T(8,128)(2,1)S(1)}, bf16[16,32,128]{2,1,0:T(8,128)(2,1)S(1)}, u32[]{:S(2)}, u32[]{:S(2)}) collective-permute-start(bf16[16,32,128]{2,1,0:T(8,128)(2,1)S(1)} %all-to-all-done.mine), channel_id=1, source_target_pairs={{1,0},{0,1},{3,2},{2,3},{5,4},{4,5},{7,6},{6,7},{9,8},{8,9},{11,10... | collective-permute-start | bytes 393224 | tf_op jit(solution)/shard_map/ppermute | solution.py:277
  47.6 10.5 %collective-permute-start.2 = (bf16[16,32,128]{2,1,0:T(8,128)(2,1)S(1)}, bf16[16,32,128]{2,1,0:T(8,128)(2,1)S(1)}, u32[]{:S(2)}, u32[]{:S(2)}) collective-permute-start(bf16[16,32,128]{2,1,0:T(8,128)(2,1)S(1)} %all-to-all-done.mine), channel_id=1, source_target_pairs={{33,0},{32,1},{35,2},{34,3},{37,4},{36,5},{39,6},{38,7},{41,8},{40... | collective-permute-start | bytes 393224 | tf_op jit(solution)/shard_map/ppermute | solution.py:277
  64.4 10.1 %collective-permute-start.3 = (bf16[32,32,128]{2,1,0:T(8,128)(2,1)S(1)}, bf16[32,32,128]{2,1,0:T(8,128)(2,1)S(1)}, u32[]{:S(2)}, u32[]{:S(2)}) collective-permute-start(bf16[32,32,128]{2,1,0:T(8,128)(2,1)S(1)} %get-tuple-element.9), channel_id=1, source_target_pairs={{0,32},{1,33},{2,34},{3,35},{4,36},{5,37},{6,38},{7,39},{8,40},{9,... | collective-permute-start | bytes 786440 | tf_op jit(solution)/shard_map/ppermute | solution.py:277

commit v3 on v2

--- a/solution.py
+++ b/solution.py
@@ -11,6 +11,8 @@
 from jax.sharding import PartitionSpec as P
 
 BATCH = 16
+GROUP = 8
+SKEW = 1
 CHUNK = 16
 META_ROWS = 16
 
@@ -36,6 +38,25 @@
     fr, fi = rounded(fresnel.real), rounded(fresnel.imag)
     dr, di = rounded(wave.real), rounded(-wave.imag)
     return np.stack([left(fr, fi), right(fr, fi), left(dr, di), right(dr, di)])
+
+
+def spread_kernel(real, imag, out):
+    parts = [ref[s] for ref in (real, imag) for s in range(real.shape[0])]
+    joined = jnp.concatenate(parts, axis=0).astype(jnp.bfloat16)
+    for z in range(out.shape[0]):
+        out[z] = joined
+
+
+def spread(real, imag, copies):
+    vmem = pl.BlockSpec(memory_space=pltpu.VMEM)
+    slices, strip, width = real.shape
+    return pl.pallas_call(
+        spread_kernel,
+        out_shape=jax.ShapeDtypeStruct((copies, 2 * slices * strip, width), jnp.bfloat16),
+        in_specs=[vmem, vmem],
+        out_specs=vmem,
+        name="spread",
+    )(real, imag)
 
 
 def pack_kernel(slots, counts, coords, patterns, out, *, n_tile, cap, tile_width, row_max):
@@ -91,6 +112,7 @@
     field,
     wave,
     rolled,
+    cut,
     *,
     cap,
 ):
@@ -133,8 +155,8 @@
     dot = functools.partial(jnp.dot, preferred_element_type=f32)
     chunks = range(0, edge, CHUNK)
 
-    def transform(left, right):
-        for b in range(0, BATCH, 2):
+    def apply_left(group, left):
+        for b in range(group * GROUP, (group + 1) * GROUP, 2):
             full = dot(tables[left], data[:, b * edge : (b + 2) * edge]).astype(bf16)
             for h in range(2):
                 for k in range(2):
@@ -142,9 +164,9 @@
                         k * edge : (k + 1) * edge, h * edge : (h + 1) * edge
                     ]
 
-    def finish(right, target):
-        for b in range(0, BATCH, 2):
-            target[b * edge : (b + 2) * edge, :] = dot(half[b * edge : (b + 2) * edge, :], tables[right])
+    def apply_right(group, right, target):
+        at = group * GROUP * edge
+        target[at : at + GROUP * edge, :] = dot(half[at : at + GROUP * edge, :], tables[right])
 
     def times(a, b):
         return (a[0] * b[0] - a[1] * b[1], a[0] * b[1] + a[1] * b[0])
@@ -159,6 +181,9 @@
     def read(ref, b, r):
         at = b * edge + r
         return (ref[at : at + CHUNK, :edge], ref[at : at + CHUNK, edge:])
+
+    def members(group):
+        return range(group * GROUP, (group + 1) * GROUP)
 
     def run_batch(i, carry):
         picks = []
@@ -186,45 +211,71 @@
             _, _, row, _, _, mask = picks[b]
             for part in range(2):
                 for h in range(2):
-                    piece = jnp.where(mask, term[part], 0.0) if h == 0 else jnp.where(mask, 0.0, term[part])
-                    acc[part * 2 + s, h, pl.ds(row + r, CHUNK), :] += piece
-
-        for b in range(BATCH):
-            shift = lax.rem(picks[b][3], edge)
-            for r in chunks:
-                at = b * edge + r
-                re = pltpu.roll(probe[0, r : r + CHUNK, :], shift, 1)
-                im = pltpu.roll(probe[1, r : r + CHUNK, :], shift, 1)
-                rolled[at : at + CHUNK, :edge] = re
-                rolled[at : at + CHUNK, edge:] = im
-                keep(b, r, times((re, im), window(b, 0, r)))
-        transform(0, 1)
-        finish(1, wave)
-        for b in range(BATCH):
-            for r in chunks:
-                keep(b, r, times(read(wave, b, r), window(b, 1, r)))
-        transform(2, 3)
-        finish(3, field)
-        for b in range(BATCH):
-            src, c, _, _, weight, _ = picks[b]
-            for r in chunks:
-                re, im = read(field, b, r)
-                start = pl.multiple_of(c * edge + r, CHUNK)
-                measured = payload[src, pl.ds(start, CHUNK), :].astype(f32)
-                excess = weight * (re * re + im * im - measured)
-                keep(b, r, (excess * re, excess * im))
-        transform(3, 2)
-        finish(2, field)
-        for b in range(BATCH):
-            for r in chunks:
-                back = read(field, b, r)
-                add_term(b, 1, r, conj_times(read(wave, b, r), back))
-                keep(b, r, conj_times(window(b, 1, r), back))
-        transform(1, 0)
-        finish(0, field)
-        for b in range(BATCH):
-            for r in chunks:
-                add_term(b, 0, r, conj_times(read(rolled, b, r), read(field, b, r)))
+                    spot = acc.at[part * 2 + s, h, pl.ds(row + r, CHUNK), :]
+                    pltpu.store(spot, spot[...] + term[part], mask=mask if h == 0 else ~mask)
+
+        def enter(group):
+            for b in members(group):
+                shift = lax.rem(picks[b][3], edge)
+                for r in chunks:
+                    at = b * edge + r
+                    re = pltpu.roll(probe[0, r : r + CHUNK, :], shift, 1)
+                    im = pltpu.roll(probe[1, r : r + CHUNK, :], shift, 1)
+                    rolled[at : at + CHUNK, :edge] = re
+                    rolled[at : at + CHUNK, edge:] = im
+                    keep(b, r, times((re, im), window(b, 0, r)))
+
+        def leave(group):
+            for b in members(group):
+                for r in chunks:
+                    at = b * edge + r
+                    slab_part = window(b, 1, r)
+                    cut[at : at + CHUNK, :edge] = slab_part[0]
+                    cut[at : at + CHUNK, edge:] = slab_part[1]
+                    keep(b, r, times(read(wave, b, r), slab_part))
+
+        def compare(group):
+            for b in members(group):
+                src, c, _, _, weight, _ = picks[b]
+                for r in chunks:
+                    re, im = read(field, b, r)
+                    start = pl.multiple_of(c * edge + r, CHUNK)
+                    measured = payload[src, pl.ds(start, CHUNK), :].astype(f32)
+                    excess = weight * (re * re + im * im - measured)
+                    keep(b, r, (excess * re, excess * im))
+
+        def turn(group):
+            for b in members(group):
+                for r in chunks:
+                    back = read(field, b, r)
+                    add_term(b, 1, r, conj_times(read(wave, b, r), back))
+                    keep(b, r, conj_times(read(cut, b, r), back))
+
+        def close(group):
+            for b in members(group):
+                for r in chunks:
+                    add_term(b, 0, r, conj_times(read(rolled, b, r), read(field, b, r)))
+
+        steps = (
+            enter,
+            lambda g: apply_left(g, 0),
+            lambda g: apply_right(g, 1, wave),
+            leave,
+            lambda g: apply_left(g, 2),
+            lambda g: apply_right(g, 3, field),
+            compare,
+            lambda g: apply_left(g, 3),
+            lambda g: apply_right(g, 2, field),
+            turn,
+            lambda g: apply_left(g, 1),
+            lambda g: apply_right(g, 0, field),
+            close,
+        )
+        n_groups = BATCH // GROUP
+        for t in range(len(steps) + (n_groups - 1) * SKEW):
+            for g in range(n_groups):
+                if 0 <= t - g * SKEW < len(steps):
+                    steps[t - g * SKEW](g)
         return carry
 
     lax.fori_loop(0, (n_live + BATCH - 1) // BATCH, run_batch, 0)
@@ -260,6 +311,7 @@
             pltpu.VMEM((BATCH * edge, 2 * edge), jnp.float32),
             pltpu.VMEM((BATCH * edge, 2 * edge), jnp.float32),
             pltpu.VMEM((BATCH * edge, 2 * edge), jnp.float32),
+            pltpu.VMEM((BATCH * edge, 2 * edge), jnp.float32),
         ],
         compiler_params=pltpu.CompilerParams(vmem_limit_bytes=48 * 1024 * 1024),
         name="local_gradient",
@@ -286,9 +338,7 @@
     per_source = patterns.shape[0]
     cap = send_slots.shape[2]
 
-    local = jnp.concatenate([object_real, object_imag]).astype(jnp.bfloat16)
-    local = local.reshape(2 * slices * strip, tile_width)
-    sent = jnp.broadcast_to(local[None], (n_pos // 2, *local.shape))
+    sent = spread(object_real, object_imag, n_pos // 2)
     same_y = [[2 * z + y for z in range(n_pos // 2)] for y in range(2)]
     mine = lax.all_to_all(sent, "pos", 0, 0, axis_index_groups=same_y, tiled=True)
 

time: 107 us -> 105 us (0.981)
  blocking collectives: 31 us -> 27.3 us
  waiting for transfers between devices: 28.3 us -> 31.2 us
  other arithmetic: 1.56 us -> 0.16 us
    all_to_all x1, blocking collectives: 31 us -> 27.3 us  [body(): pieces = lax.all_to_all(total.astype(jnp.bfloat16), 'pos', 0, 0, tiled=True)]
    ppermute x4, waiting for transfers between devices: 8.82 us -> 11.7 us  [moved(): return lax.ppermute(value, ('tile', 'pos'), pairs)]
    another operation x2 -> x0, other arithmetic: 1.4 us -> none
    pallas_call x0 -> x1, Pallas kernels: none -> 1.38 us  [spread(): pl.pallas_call(spread_kernel, out_shape=jax.ShapeDtypeStruct((copies, 2 *...]
where the time goes in v3:
time: 105 us; the launch traced here: 104 us
  starting transfers between devices  34.7 us (33%)
  waiting for transfers between devices  31.2 us (30%)
  blocking collectives  27.3 us (26%)
  Pallas kernels  9.25 us (9%)
    all_to_all x1, blocking collectives, body(): pieces = lax.all_to_all(total.astype(jnp.bfloat16), 'pos', 0, 0, tiled=True)  27.3 us
    all_to_all x1, starting transfers between devices, body(): lax.all_to_all(sent, 'pos', 0, 0, axis_index_groups=same_y, tiled=True)  15.2 us
    all_to_all x1, waiting for transfers between devices, body(): lax.all_to_all(sent, 'pos', 0, 0, axis_index_groups=same_y, tiled=True)  12.4 us
    ppermute x4, starting transfers between devices, moved(): return lax.ppermute(value, ('tile', 'pos'), pairs)  12.1 us
    ppermute x4, waiting for transfers between devices, moved(): return lax.ppermute(value, ('tile', 'pos'), pairs)  11.7 us
    all_to_all x1, starting transfers between devices, body(): payload = lax.all_to_all(payload, 'tile', 0, 0, tiled=True)  7.43 us
    all_to_all x1, waiting for transfers between devices, body(): payload = lax.all_to_all(payload, 'tile', 0, 0, tiled=True)  7.05 us
    pallas_call x1, Pallas kernels, local_gradient(): pl.pallas_call(functools.partial(grad_kernel, cap=cap), out_shape=(share,...  5.61 us
  transfers between devices with their start and end apart: 6, of which 5 were waited for; matrix products, arithmetic and copies ran while one was open for 0% of the time, Pallas kernels for 2%

profile of v3, /device:TPU:6, one launch (start us, length us, event | category | flops | bytes accessed | tf_op | source)
XLA Modules:
  0.0 103.9 jit_solution(8257185403605072426)
XLA Ops:
  0.6 1.4 %spread.1 = bf16[16,32,128]{2,1,0:T(8,128)(2,1)} custom-call(f32[2,8,128]{2,1,0:T(8,128)} %real.1, f32[2,8,128]{2,1,0:T(8,128)} %imag.1), custom_call_target="tpu_custom_call" | custom-call | tf_op jit(solution)/shard_map/spread/pallas_call | solution.py:53
  2.0 15.2 %all-to-all-start = ((bf16[16,32,128]{2,1,0:T(8,128)(2,1)}), bf16[16,32,128]{2,1,0:T(8,128)(2,1)S(1)}, u32[]{:S(2)}, u32[]{:S(2)}) async-start(bf16[16,32,128]{2,1,0:T(8,128)(2,1)} %spread.1), calls=%async_computation | async-start | bytes 262144 | tf_op jit(solution)/shard_map/all_to_all | solution.py:343
  17.2 2.3 %pack.1 = bf16[16,272,128]{2,1,0:T(8,128)(2,1)} custom-call(s32[2,16]{1,0:T(2,128)} %bitcast.15, s32[1,16]{1,0:T(1,128)} %counts.1, s32[2,16]{1,0:T(2,128)} %bitcast.16, bf16[16,128,128]{2,1,0:T(8,128)(2,1)} %patterns.1), custom_call_target="tpu_custom_call" | custom-call | tf_op jit(solution)/shard_map/pack/pallas_call | solution.py:86
  19.5 0.0 copy-start.1
  19.5 0.0 copy-start.2
  19.5 0.0 copy-start
  19.5 12.4 %all-to-all-done.mine = bf16[16,32,128]{2,1,0:T(8,128)(2,1)S(1)} async-done(((bf16[16,32,128]{2,1,0:T(8,128)(2,1)}), bf16[16,32,128]{2,1,0:T(8,128)(2,1)S(1)}, u32[]{:S(2)}, u32[]{:S(2)}) %all-to-all-start) | async-done | bytes 131104 | tf_op jit(solution)/shard_map/all_to_all | solution.py:343
  31.9 7.4 %all-to-all-start.1 = ((bf16[16,272,128]{2,1,0:T(8,128)(2,1)}), bf16[16,272,128]{2,1,0:T(8,128)(2,1)S(1)}, u32[]{:S(2)}, u32[]{:S(2)}) async-start(bf16[16,272,128]{2,1,0:T(8,128)(2,1)} %pack.1), calls=%async_computation.1 | async-start | bytes 2228224 | tf_op jit(solution)/shard_map/all_to_all | solution.py:356
  39.3 0.0 copy-done.1
  39.3 0.0 copy-done.2
  39.4 4.9 %collective-permute-start = (bf16[16,32,128]{2,1,0:T(8,128)(2,1)S(1)}, bf16[16,32,128]{2,1,0:T(8,128)(2,1)S(1)}, u32[]{:S(2)}, u32[]{:S(2)}) collective-permute-start(bf16[16,32,128]{2,1,0:T(8,128)(2,1)S(1)} %all-to-all-done.mine), channel_id=1, source_target_pairs={{32,0},{33,1},{34,2},{35,3},{36,4},{37,5},{38,6},{39,7},{40,8},{41... | collective-permute-start | bytes 393224 | tf_op jit(solution)/shard_map/ppermute | solution.py:329
  44.3 2.6 %collective-permute-start.1 = (bf16[16,32,128]{2,1,0:T(8,128)(2,1)S(1)}, bf16[16,32,128]{2,1,0:T(8,128)(2,1)S(1)}, u32[]{:S(2)}, u32[]{:S(2)}) collective-permute-start(bf16[16,32,128]{2,1,0:T(8,128)(2,1)S(1)} %all-to-all-done.mine), channel_id=1, source_target_pairs={{1,0},{0,1},{3,2},{2,3},{5,4},{4,5},{7,6},{6,7},{9,8},{8,9},{11,10... | collective-permute-start | bytes 393224 | tf_op jit(solution)/shard_map/ppermute | solution.py:329
  46.9 1.9 %collective-permute-start.2 = (bf16[16,32,128]{2,1,0:T(8,128)(2,1)S(1)}, bf16[16,32,128]{2,1,0:T(8,128)(2,1)S(1)}, u32[]{:S(2)}, u32[]{:S(2)}) collective-permute-start(bf16[16,32,128]{2,1,0:T(8,128)(2,1)S(1)} %all-to-all-done.mine), channel_id=1, source_target_pairs={{33,0},{32,1},{35,2},{34,3},{37,4},{36,5},{39,6},{38,7},{41,8},{40... | collective-permute-start | bytes 393224 | tf_op jit(solution)/shard_map/ppermute | solution.py:329
  48.8 7.1 %all-to-all-done.1.payload = bf16[16,272,128]{2,1,0:T(8,128)(2,1)S(1)} async-done(((bf16[16,272,128]{2,1,0:T(8,128)(2,1)}), bf16[16,272,128]{2,1,0:T(8,128)(2,1)S(1)}, u32[]{:S(2)}, u32[]{:S(2)}) %all-to-all-start.1) | async-done | bytes 1114144 | tf_op jit(solution)/shard_map/all_to_all | solution.py:356
  55.9 0.0 collective-permute-done.mine_next
  55.9 0.5 collective-permute-done.1.other
  56.4 0.9 collective-permute-done.2.other_next
  57.4 0.0 copy-done
  57.4 5.6 %local_gradient.1 = (bf16[32,32,128]{2,1,0:T(8,128)(2,1)S(1)}, bf16[32,32,128]{2,1,0:T(8,128)(2,1)S(1)}) custom-call(s32[1]{0:T(128)} %bitcast.here, s32[16,128]{1,0:T(8,128)S(1)} %bitcast.12, bf16[16,272,128]{2,1,0:T(8,128)(2,1)S(1)} %all-to-all-done.1.payload, bf16[16,32,128]{2,1,0:T(8,128)(2,1)S(1)} %all-to-all-done.mine, ...), custom_call_target="tpu_custom_call" | custom-call | tf_op jit(solution)/shard_map/local_gradient/pallas_call | solution.py:300
  63.0 2.7 %collective-permute-start.3 = (bf16[32,32,128]{2,1,0:T(8,128)(2,1)S(1)}, bf16[32,32,128]{2,1,0:T(8,128)(2,1)S(1)}, u32[]{:S(2)}, u32[]{:S(2)}) collective-permute-start(bf16[32,32,128]{2,1,0:T(8,128)(2,1)S(1)} %get-tuple-element.9), channel_id=1, source_target_pairs={{0,32},{1,33},{2,34},{3,35},{4,36},{5,37},{6,38},{7,39},{8,40},{9,... | collective-permute-start | bytes 786440 | tf_op jit(solution)/shard_map/ppermute | solution.py:329
  65.7 10.2 %collective-permute-done.3 = bf16[32,32,128]{2,1,0:T(8,128)(2,1)S(1)} collective-permute-done((bf16[32,32,128]{2,1,0:T(8,128)(2,1)S(1)}, bf16[32,32,128]{2,1,0:T(8,128)(2,1)S(1)}, u32[]{:S(2)}, u32[]{:S(2)}) %collective-permute-start.3) | collective-permute-done | bytes 262176 | tf_op jit(solution)/shard_map/ppermute | solution.py:329
  75.9 0.1 add_convert_fusion
  76.0 27.3 %all_to_all.15 = bf16[32,32,128]{2,1,0:T(8,128)(2,1)S(1)} all-to-all(bf16[32,32,128]{2,1,0:T(8,128)(2,1)S(1)} %add_convert_fusion), channel_id=1, replica_groups=mesh['tile'=16,'pos'=32] {'pos'}, dimensions={0} | all-to-all | bytes 524288 | tf_op jit(solution)/shard_map/all_to_all | solution.py:369
  103.3 0.6 slice_bitcast_fusion
  (4 shorter events, 0.1 us)
Async XLA Ops:
  2.0 29.9 %all-to-all-start = ((bf16[16,32,128]{2,1,0:T(8,128)(2,1)}), bf16[16,32,128]{2,1,0:T(8,128)(2,1)S(1)}, u32[]{:S(2)}, u32[]{:S(2)}) async-start(bf16[16,32,128]{2,1,0:T(8,128)(2,1)} %spread.1), calls=%async_computation | async-start | bytes 262144 | tf_op jit(solution)/shard_map/all_to_all | solution.py:343
  19.5 19.9 %copy-start.1 = (f32[128,128]{1,0:T(8,128)S(1)}, f32[128,128]{1,0:T(8,128)}, u32[]{:S(2)}) copy-start(f32[128,128]{1,0:T(8,128)} %param.16) | copy-start | bytes 196612
  19.5 19.9 %copy-start.2 = (f32[128,128]{1,0:T(8,128)S(1)}, f32[128,128]{1,0:T(8,128)}, u32[]{:S(2)}) copy-start(f32[128,128]{1,0:T(8,128)} %param.15) | copy-start | bytes 196612
  19.5 37.9 %copy-start = (bf16[4,256,256]{2,1,0:T(8,128)(2,1)S(1)}, bf16[4,256,256]{2,1,0:T(8,128)(2,1)}, u32[]{:S(2)}) copy-start(bf16[4,256,256]{2,1,0:T(8,128)(2,1)} %constant.23.clone.tables) | copy-start | bytes 1572868
  31.9 24.0 %all-to-all-start.1 = ((bf16[16,272,128]{2,1,0:T(8,128)(2,1)}), bf16[16,272,128]{2,1,0:T(8,128)(2,1)S(1)}, u32[]{:S(2)}, u32[]{:S(2)}) async-start(bf16[16,272,128]{2,1,0:T(8,128)(2,1)} %pack.1), calls=%async_computation.1 | async-start | bytes 2228224 | tf_op jit(solution)/shard_map/all_to_all | solution.py:356
  39.4 16.5 %collective-permute-start = (bf16[16,32,128]{2,1,0:T(8,128)(2,1)S(1)}, bf16[16,32,128]{2,1,0:T(8,128)(2,1)S(1)}, u32[]{:S(2)}, u32[]{:S(2)}) collective-permute-start(bf16[16,32,128]{2,1,0:T(8,128)(2,1)S(1)} %all-to-all-done.mine), channel_id=1, source_target_pairs={{32,0},{33,1},{34,2},{35,3},{36,4},{37,5},{38,6},{39,7},{40,8},{41... | collective-permute-start | bytes 393224 | tf_op jit(solution)/shard_map/ppermute | solution.py:329
  44.3 12.1 %collective-permute-start.1 = (bf16[16,32,128]{2,1,0:T(8,128)(2,1)S(1)}, bf16[16,32,128]{2,1,0:T(8,128)(2,1)S(1)}, u32[]{:S(2)}, u32[]{:S(2)}) collective-permute-start(bf16[16,32,128]{2,1,0:T(8,128)(2,1)S(1)} %all-to-all-done.mine), channel_id=1, source_target_pairs={{1,0},{0,1},{3,2},{2,3},{5,4},{4,5},{7,6},{6,7},{9,8},{8,9},{11,10... | collective-permute-start | bytes 393224 | tf_op jit(solution)/shard_map/ppermute | solution.py:329
  46.9 10.5 %collective-permute-start.2 = (bf16[16,32,128]{2,1,0:T(8,128)(2,1)S(1)}, bf16[16,32,128]{2,1,0:T(8,128)(2,1)S(1)}, u32[]{:S(2)}, u32[]{:S(2)}) collective-permute-start(bf16[16,32,128]{2,1,0:T(8,128)(2,1)S(1)} %all-to-all-done.mine), channel_id=1, source_target_pairs={{33,0},{32,1},{35,2},{34,3},{37,4},{36,5},{39,6},{38,7},{41,8},{40... | collective-permute-start | bytes 393224 | tf_op jit(solution)/shard_map/ppermute | solution.py:329
  63.0 12.9 %collective-permute-start.3 = (bf16[32,32,128]{2,1,0:T(8,128)(2,1)S(1)}, bf16[32,32,128]{2,1,0:T(8,128)(2,1)S(1)}, u32[]{:S(2)}, u32[]{:S(2)}) collective-permute-start(bf16[32,32,128]{2,1,0:T(8,128)(2,1)S(1)} %get-tuple-element.9), channel_id=1, source_target_pairs={{0,32},{1,33},{2,34},{3,35},{4,36},{5,37},{6,38},{7,39},{8,40},{9,... | collective-permute-start | bytes 786440 | tf_op jit(solution)/shard_map/ppermute | solution.py:329

commit v4 on v3

--- a/solution.py
+++ b/solution.py
@@ -351,8 +351,9 @@
         tile_width,
         n_pos * strip - edge_len,
     )
-    mine, payload = lax.optimization_barrier((mine, payload))
-    strips = (mine, moved(mine, 1, False), moved(mine, 0, True), moved(mine, 1, True))
+    other = moved(mine, 0, True)
+    other, payload = lax.optimization_barrier((other, payload))
+    strips = (mine, moved(mine, 1, False), other, moved(other, 1, False))
     payload = lax.all_to_all(payload, "tile", 0, 0, tiled=True)
     meta = payload[:, cap * edge_len, :].astype(jnp.int32)
 

time: 105 us -> 108 us (1.029)
  blocking collectives: 27.3 us -> 53 us
  starting transfers between devices: 34.7 us -> 20 us
  waiting for transfers between devices: 31.2 us -> 18.5 us
  Pallas kernels: 9.25 us -> 13.4 us
    all_to_all x0 -> x1, blocking collectives: none -> 29.9 us  [body(): lax.all_to_all(sent, 'pos', 0, 0, axis_index_groups=same_y, tiled=True)]
    all_to_all x1 -> x0, starting transfers between devices: 15.2 us -> none  [body(): lax.all_to_all(sent, 'pos', 0, 0, axis_index_groups=same_y, tiled=True)]
    all_to_all x1 -> x0, waiting for transfers between devices: 12.4 us -> none  [body(): lax.all_to_all(sent, 'pos', 0, 0, axis_index_groups=same_y, tiled=True)]
    all_to_all x1, blocking collectives: 27.3 us -> 23.1 us  [body(): pieces = lax.all_to_all(total.astype(jnp.bfloat16), 'pos', 0, 0, tiled=True)]
    pallas_call x1, Pallas kernels: 5.61 us -> 9.74 us  [local_gradient(): pl.pallas_call(functools.partial(grad_kernel, cap=cap), out_shape=(share,...]
    ppermute x4, waiting for transfers between devices: 11.7 us -> 9.28 us  [moved(): return lax.ppermute(value, ('tile', 'pos'), pairs)]
    all_to_all x1, waiting for transfers between devices: 7.05 us -> 9.25 us  [body(): payload = lax.all_to_all(payload, 'tile', 0, 0, tiled=True)]
  transfers between devices with their start and end apart: 6 -> 5, of which waited for: 5 -> 3; matrix products, arithmetic and copies ran while one was open for 0% -> 0% of each run, Pallas kernels for 2% -> 2%
where the time goes in v4:
time: 108 us; the launch traced here: 106 us
  blocking collectives  53 us (49%)
  starting transfers between devices  20 us (19%)
  waiting for transfers between devices  18.5 us (17%)
  Pallas kernels  13.4 us (12%)
    all_to_all x1, blocking collectives, body(): lax.all_to_all(sent, 'pos', 0, 0, axis_index_groups=same_y, tiled=True)  29.9 us
    all_to_all x1, blocking collectives, body(): pieces = lax.all_to_all(total.astype(jnp.bfloat16), 'pos', 0, 0, tiled=True)  23.1 us
    ppermute x4, starting transfers between devices, moved(): return lax.ppermute(value, ('tile', 'pos'), pairs)  12.6 us
    pallas_call x1, Pallas kernels, local_gradient(): pl.pallas_call(functools.partial(grad_kernel, cap=cap), out_shape=(share,...  9.74 us
    ppermute x4, waiting for transfers between devices, moved(): return lax.ppermute(value, ('tile', 'pos'), pairs)  9.28 us
    all_to_all x1, waiting for transfers between devices, body(): payload = lax.all_to_all(payload, 'tile', 0, 0, tiled=True)  9.25 us
    all_to_all x1, starting transfers between devices, body(): payload = lax.all_to_all(payload, 'tile', 0, 0, tiled=True)  7.43 us
    pallas_call x1, Pallas kernels, pack(): pl.pallas_call(body, out_shape=jax.ShapeDtypeStruct((n_tile, cap * rows +...  2.26 us
  transfers between devices with their start and end apart: 5, of which 3 were waited for; matrix products, arithmetic and copies ran while one was open for 0% of the time, Pallas kernels for 2%

profile of v4, /device:TPU:6, one launch (start us, length us, event | category | flops | bytes accessed | tf_op | source)
XLA Modules:
  0.0 106.4 jit_solution(17038868706456897196)
XLA Ops:
  0.6 1.4 %spread.1 = bf16[16,32,128]{2,1,0:T(8,128)(2,1)} custom-call(f32[2,8,128]{2,1,0:T(8,128)} %real.1, f32[2,8,128]{2,1,0:T(8,128)} %imag.1), custom_call_target="tpu_custom_call" | custom-call | tf_op jit(solution)/shard_map/spread/pallas_call | solution.py:53
  2.0 29.9 %all_to_all.15.mine = bf16[16,32,128]{2,1,0:T(8,128)(2,1)S(1)} all-to-all(bf16[16,32,128]{2,1,0:T(8,128)(2,1)} %spread.1), channel_id=1, replica_groups={{0,2,4,6,8,10,12,14,16,18,20,22,24,26,28,30},{1,3,5,7,9,11,13,15,17,19,..., dimensions={0} | all-to-all | bytes 262144 | tf_op jit(solution)/shard_map/all_to_all | solution.py:343
  31.9 3.5 %collective-permute-start = (bf16[16,32,128]{2,1,0:T(8,128)(2,1)S(1)}, bf16[16,32,128]{2,1,0:T(8,128)(2,1)S(1)}, u32[]{:S(2)}, u32[]{:S(2)}) collective-permute-start(bf16[16,32,128]{2,1,0:T(8,128)(2,1)S(1)} %all_to_all.15.mine), channel_id=1, source_target_pairs={{1,0},{0,1},{3,2},{2,3},{5,4},{4,5},{7,6},{6,7},{9,8},{8,9},{11,10... | collective-permute-start | bytes 393224 | tf_op jit(solution)/shard_map/ppermute | solution.py:329
  35.4 2.3 %pack.1 = bf16[16,272,128]{2,1,0:T(8,128)(2,1)} custom-call(s32[2,16]{1,0:T(2,128)} %bitcast.15, s32[1,16]{1,0:T(1,128)} %counts.1, s32[2,16]{1,0:T(2,128)} %bitcast.16, bf16[16,128,128]{2,1,0:T(8,128)(2,1)} %patterns.1), custom_call_target="tpu_custom_call" | custom-call | tf_op jit(solution)/shard_map/pack/pallas_call | solution.py:86
  37.6 0.0 copy-start.1
  37.6 0.0 copy-start.2
  37.6 0.0 copy-start
  37.6 1.1 %collective-permute-done.other = bf16[16,32,128]{2,1,0:T(8,128)(2,1)S(1)} collective-permute-done((bf16[16,32,128]{2,1,0:T(8,128)(2,1)S(1)}, bf16[16,32,128]{2,1,0:T(8,128)(2,1)S(1)}, u32[]{:S(2)}, u32[]{:S(2)}) %collective-permute-start) | collective-permute-done | bytes 131104 | tf_op jit(solution)/shard_map/ppermute | solution.py:329
  38.7 7.4 %all-to-all-start.1 = ((bf16[16,272,128]{2,1,0:T(8,128)(2,1)}), bf16[16,272,128]{2,1,0:T(8,128)(2,1)S(1)}, u32[]{:S(2)}, u32[]{:S(2)}) async-start(bf16[16,272,128]{2,1,0:T(8,128)(2,1)} %pack.1), calls=%async_computation.1 | async-start | bytes 2228224 | tf_op jit(solution)/shard_map/all_to_all | solution.py:357
  46.2 0.0 copy-done.1
  46.2 0.0 copy-done.2
  46.2 4.9 %collective-permute-start.1 = (bf16[16,32,128]{2,1,0:T(8,128)(2,1)S(1)}, bf16[16,32,128]{2,1,0:T(8,128)(2,1)S(1)}, u32[]{:S(2)}, u32[]{:S(2)}) collective-permute-start(bf16[16,32,128]{2,1,0:T(8,128)(2,1)S(1)} %all_to_all.15.mine), channel_id=1, source_target_pairs={{32,0},{33,1},{34,2},{35,3},{36,4},{37,5},{38,6},{39,7},{40,8},{41... | collective-permute-start | bytes 393224 | tf_op jit(solution)/shard_map/ppermute | solution.py:329
  51.1 2.3 %collective-permute-start.2 = (bf16[16,32,128]{2,1,0:T(8,128)(2,1)S(1)}, bf16[16,32,128]{2,1,0:T(8,128)(2,1)S(1)}, u32[]{:S(2)}, u32[]{:S(2)}) collective-permute-start(bf16[16,32,128]{2,1,0:T(8,128)(2,1)S(1)} %collective-permute-done.other), channel_id=1, source_target_pairs={{32,0},{33,1},{34,2},{35,3},{36,4},{37,5},{38,6},{39,7},{40,8},{41... | collective-permute-start | bytes 393224 | tf_op jit(solution)/shard_map/ppermute | solution.py:329
  53.4 9.2 %all-to-all-done.1.payload = bf16[16,272,128]{2,1,0:T(8,128)(2,1)S(1)} async-done(((bf16[16,272,128]{2,1,0:T(8,128)(2,1)}), bf16[16,272,128]{2,1,0:T(8,128)(2,1)S(1)}, u32[]{:S(2)}, u32[]{:S(2)}) %all-to-all-start.1) | async-done | bytes 1114144 | tf_op jit(solution)/shard_map/all_to_all | solution.py:357
  62.7 0.0 collective-permute-done.1.mine_next
  62.7 0.0 collective-permute-done.2.other_next
  62.7 0.0 copy-done
  62.7 9.7 %local_gradient.1 = (bf16[32,32,128]{2,1,0:T(8,128)(2,1)S(1)}, bf16[32,32,128]{2,1,0:T(8,128)(2,1)S(1)}) custom-call(s32[1]{0:T(128)} %bitcast.here, s32[16,128]{1,0:T(8,128)S(1)} %bitcast.12, bf16[16,272,128]{2,1,0:T(8,128)(2,1)S(1)} %all-to-all-done.1.payload, bf16[16,32,128]{2,1,0:T(8,128)(2,1)S(1)} %all_to_all.15.mine, ...), custom_call_target="tpu_custom_call" | custom-call | tf_op jit(solution)/shard_map/local_gradient/pallas_call | solution.py:300
  72.5 1.9 %collective-permute-start.3 = (bf16[32,32,128]{2,1,0:T(8,128)(2,1)S(1)}, bf16[32,32,128]{2,1,0:T(8,128)(2,1)S(1)}, u32[]{:S(2)}, u32[]{:S(2)}) collective-permute-start(bf16[32,32,128]{2,1,0:T(8,128)(2,1)S(1)} %get-tuple-element.9), channel_id=1, source_target_pairs={{0,32},{1,33},{2,34},{3,35},{4,36},{5,37},{6,38},{7,39},{8,40},{9,... | collective-permute-start | bytes 786440 | tf_op jit(solution)/shard_map/ppermute | solution.py:329
  74.4 8.2 %collective-permute-done.3 = bf16[32,32,128]{2,1,0:T(8,128)(2,1)S(1)} collective-permute-done((bf16[32,32,128]{2,1,0:T(8,128)(2,1)S(1)}, bf16[32,32,128]{2,1,0:T(8,128)(2,1)S(1)}, u32[]{:S(2)}, u32[]{:S(2)}) %collective-permute-start.3) | collective-permute-done | bytes 262176 | tf_op jit(solution)/shard_map/ppermute | solution.py:329
  82.6 0.1 add_convert_fusion
  82.6 23.1 %all_to_all.16 = bf16[32,32,128]{2,1,0:T(8,128)(2,1)S(1)} all-to-all(bf16[32,32,128]{2,1,0:T(8,128)(2,1)S(1)} %add_convert_fusion), channel_id=1, replica_groups=mesh['tile'=16,'pos'=32] {'pos'}, dimensions={0} | all-to-all | bytes 524288 | tf_op jit(solution)/shard_map/all_to_all | solution.py:370
  105.8 0.6 slice_bitcast_fusion
  (4 shorter events, 0.1 us)
Async XLA Ops:
  31.9 6.8 %collective-permute-start = (bf16[16,32,128]{2,1,0:T(8,128)(2,1)S(1)}, bf16[16,32,128]{2,1,0:T(8,128)(2,1)S(1)}, u32[]{:S(2)}, u32[]{:S(2)}) collective-permute-start(bf16[16,32,128]{2,1,0:T(8,128)(2,1)S(1)} %all_to_all.15.mine), channel_id=1, source_target_pairs={{1,0},{0,1},{3,2},{2,3},{5,4},{4,5},{7,6},{6,7},{9,8},{8,9},{11,10... | collective-permute-start | bytes 393224 | tf_op jit(solution)/shard_map/ppermute | solution.py:329
  37.6 8.5 %copy-start.1 = (f32[128,128]{1,0:T(8,128)S(1)}, f32[128,128]{1,0:T(8,128)}, u32[]{:S(2)}) copy-start(f32[128,128]{1,0:T(8,128)} %param.16) | copy-start | bytes 196612
  37.6 8.5 %copy-start.2 = (f32[128,128]{1,0:T(8,128)S(1)}, f32[128,128]{1,0:T(8,128)}, u32[]{:S(2)}) copy-start(f32[128,128]{1,0:T(8,128)} %param.15) | copy-start | bytes 196612
  37.6 25.1 %copy-start = (bf16[4,256,256]{2,1,0:T(8,128)(2,1)S(1)}, bf16[4,256,256]{2,1,0:T(8,128)(2,1)}, u32[]{:S(2)}) copy-start(bf16[4,256,256]{2,1,0:T(8,128)(2,1)} %constant.23.clone.tables) | copy-start | bytes 1572868
  38.7 23.9 %all-to-all-start.1 = ((bf16[16,272,128]{2,1,0:T(8,128)(2,1)}), bf16[16,272,128]{2,1,0:T(8,128)(2,1)S(1)}, u32[]{:S(2)}, u32[]{:S(2)}) async-start(bf16[16,272,128]{2,1,0:T(8,128)(2,1)} %pack.1), calls=%async_computation.1 | async-start | bytes 2228224 | tf_op jit(solution)/shard_map/all_to_all | solution.py:357
  46.2 16.5 %collective-permute-start.1 = (bf16[16,32,128]{2,1,0:T(8,128)(2,1)S(1)}, bf16[16,32,128]{2,1,0:T(8,128)(2,1)S(1)}, u32[]{:S(2)}, u32[]{:S(2)}) collective-permute-start(bf16[16,32,128]{2,1,0:T(8,128)(2,1)S(1)} %all_to_all.15.mine), channel_id=1, source_target_pairs={{32,0},{33,1},{34,2},{35,3},{36,4},{37,5},{38,6},{39,7},{40,8},{41... | collective-permute-start | bytes 393224 | tf_op jit(solution)/shard_map/ppermute | solution.py:329
  51.1 11.6 %collective-permute-start.2 = (bf16[16,32,128]{2,1,0:T(8,128)(2,1)S(1)}, bf16[16,32,128]{2,1,0:T(8,128)(2,1)S(1)}, u32[]{:S(2)}, u32[]{:S(2)}) collective-permute-start(bf16[16,32,128]{2,1,0:T(8,128)(2,1)S(1)} %collective-permute-done.other), channel_id=1, source_target_pairs={{32,0},{33,1},{34,2},{35,3},{36,4},{37,5},{38,6},{39,7},{40,8},{41... | collective-permute-start | bytes 393224 | tf_op jit(solution)/shard_map/ppermute | solution.py:329
  72.5 10.1 %collective-permute-start.3 = (bf16[32,32,128]{2,1,0:T(8,128)(2,1)S(1)}, bf16[32,32,128]{2,1,0:T(8,128)(2,1)S(1)}, u32[]{:S(2)}, u32[]{:S(2)}) collective-permute-start(bf16[32,32,128]{2,1,0:T(8,128)(2,1)S(1)} %get-tuple-element.9), channel_id=1, source_target_pairs={{0,32},{1,33},{2,34},{3,35},{4,36},{5,37},{6,38},{7,39},{8,40},{9,... | collective-permute-start | bytes 786440 | tf_op jit(solution)/shard_map/ppermute | solution.py:329

commit v5 on v3

--- a/solution.py
+++ b/solution.py
@@ -97,9 +97,9 @@
     meta,
     payload,
     mine,
-    mine_next,
     other,
     other_next,
+    mine_next,
     tables,
     probe,
     own_out,
@@ -124,16 +124,10 @@
     for i in range(slot_count + BATCH):
         order[i] = 0
 
-    def note(i, n):
-        live = meta[i // cap, (i % cap) * 3 + 2]
-
-        @pl.when(live > 0)
-        def _():
-            order[n] = i
-
-        return n + live
-
-    n_live = lax.fori_loop(0, slot_count, note, jnp.int32(0))
+    n_live = jnp.int32(0)
+    for i in range(slot_count):
+        order[n_live] = i
+        n_live += meta[i // cap, (i % cap) * 3 + 2]
 
     def unpack(z, carry):
         for ref, y, h in (
@@ -352,7 +346,9 @@
         n_pos * strip - edge_len,
     )
     mine, payload = lax.optimization_barrier((mine, payload))
-    strips = (mine, moved(mine, 1, False), moved(mine, 0, True), moved(mine, 1, True))
+    other = moved(mine, 0, True)
+    other_next = moved(mine, 1, True)
+    strips = (mine, other, other_next, moved(mine, 1, False))
     payload = lax.all_to_all(payload, "tile", 0, 0, tiled=True)
     meta = payload[:, cap * edge_len, :].astype(jnp.int32)
 

time: 105 us -> 104 us (level)
  waiting for transfers between devices: 31.2 us -> 24.4 us
  starting transfers between devices: 34.7 us -> 38.7 us
  blocking collectives: 27.3 us -> 29.9 us
    ppermute x4, waiting for transfers between devices: 11.7 us -> 6.16 us  [moved(): return lax.ppermute(value, ('tile', 'pos'), pairs)]
    ppermute x4, starting transfers between devices: 12.1 us -> 16.1 us  [moved(): return lax.ppermute(value, ('tile', 'pos'), pairs)]
    all_to_all x1, blocking collectives: 27.3 us -> 29.9 us  [body(): pieces = lax.all_to_all(total.astype(jnp.bfloat16), 'pos', 0, 0, tiled=True)]
    all_to_all x1, waiting for transfers between devices: 7.05 us -> 5.81 us  [body(): payload = lax.all_to_all(payload, 'tile', 0, 0, tiled=True)]
where the time goes in v5:
time: 104 us; the launch traced here: 103 us
  starting transfers between devices  38.7 us (37%)
  blocking collectives  29.9 us (29%)
  waiting for transfers between devices  24.4 us (23%)
  Pallas kernels  8.64 us (8%)
    all_to_all x1, blocking collectives, body(): pieces = lax.all_to_all(total.astype(jnp.bfloat16), 'pos', 0, 0, tiled=True)  29.9 us
    ppermute x4, starting transfers between devices, moved(): return lax.ppermute(value, ('tile', 'pos'), pairs)  16.1 us
    all_to_all x1, starting transfers between devices, body(): lax.all_to_all(sent, 'pos', 0, 0, axis_index_groups=same_y, tiled=True)  15.2 us
    all_to_all x1, waiting for transfers between devices, body(): lax.all_to_all(sent, 'pos', 0, 0, axis_index_groups=same_y, tiled=True)  12.4 us
    all_to_all x1, starting transfers between devices, body(): payload = lax.all_to_all(payload, 'tile', 0, 0, tiled=True)  7.43 us
    ppermute x4, waiting for transfers between devices, moved(): return lax.ppermute(value, ('tile', 'pos'), pairs)  6.16 us
    all_to_all x1, waiting for transfers between devices, body(): payload = lax.all_to_all(payload, 'tile', 0, 0, tiled=True)  5.81 us
    pallas_call x1, Pallas kernels, local_gradient(): pl.pallas_call(functools.partial(grad_kernel, cap=cap), out_shape=(share,...  5.01 us
  transfers between devices with their start and end apart: 6, of which 5 were waited for; matrix products, arithmetic and copies ran while one was open for 0% of the time, Pallas kernels for 2%

profile of v5, /device:TPU:6, one launch (start us, length us, event | category | flops | bytes accessed | tf_op | source)
XLA Modules:
  0.0 103.1 jit_solution(13917594796598999840)
XLA Ops:
  0.6 1.4 %spread.1 = bf16[16,32,128]{2,1,0:T(8,128)(2,1)} custom-call(f32[2,8,128]{2,1,0:T(8,128)} %real.1, f32[2,8,128]{2,1,0:T(8,128)} %imag.1), custom_call_target="tpu_custom_call" | custom-call | tf_op jit(solution)/shard_map/spread/pallas_call | solution.py:53
  2.0 15.2 %all-to-all-start = ((bf16[16,32,128]{2,1,0:T(8,128)(2,1)}), bf16[16,32,128]{2,1,0:T(8,128)(2,1)S(1)}, u32[]{:S(2)}, u32[]{:S(2)}) async-start(bf16[16,32,128]{2,1,0:T(8,128)(2,1)} %spread.1), calls=%async_computation | async-start | bytes 262144 | tf_op jit(solution)/shard_map/all_to_all | solution.py:337
  17.2 2.3 %pack.1 = bf16[16,272,128]{2,1,0:T(8,128)(2,1)} custom-call(s32[2,16]{1,0:T(2,128)} %bitcast.15, s32[1,16]{1,0:T(1,128)} %counts.1, s32[2,16]{1,0:T(2,128)} %bitcast.16, bf16[16,128,128]{2,1,0:T(8,128)(2,1)} %patterns.1), custom_call_target="tpu_custom_call" | custom-call | tf_op jit(solution)/shard_map/pack/pallas_call | solution.py:86
  19.5 0.0 copy-start.1
  19.5 0.0 copy-start.2
  19.5 0.0 copy-start
  19.5 12.4 %all-to-all-done.mine = bf16[16,32,128]{2,1,0:T(8,128)(2,1)S(1)} async-done(((bf16[16,32,128]{2,1,0:T(8,128)(2,1)}), bf16[16,32,128]{2,1,0:T(8,128)(2,1)S(1)}, u32[]{:S(2)}, u32[]{:S(2)}) %all-to-all-start) | async-done | bytes 131104 | tf_op jit(solution)/shard_map/all_to_all | solution.py:337
  31.9 7.4 %all-to-all-start.1 = ((bf16[16,272,128]{2,1,0:T(8,128)(2,1)}), bf16[16,272,128]{2,1,0:T(8,128)(2,1)S(1)}, u32[]{:S(2)}, u32[]{:S(2)}) async-start(bf16[16,272,128]{2,1,0:T(8,128)(2,1)} %pack.1), calls=%async_computation.1 | async-start | bytes 2228224 | tf_op jit(solution)/shard_map/all_to_all | solution.py:352
  39.3 0.0 copy-done.1
  39.3 0.0 copy-done.2
  39.4 2.6 %collective-permute-start = (bf16[16,32,128]{2,1,0:T(8,128)(2,1)S(1)}, bf16[16,32,128]{2,1,0:T(8,128)(2,1)S(1)}, u32[]{:S(2)}, u32[]{:S(2)}) collective-permute-start(bf16[16,32,128]{2,1,0:T(8,128)(2,1)S(1)} %all-to-all-done.mine), channel_id=1, source_target_pairs={{1,0},{0,1},{3,2},{2,3},{5,4},{4,5},{7,6},{6,7},{9,8},{8,9},{11,10... | collective-permute-start | bytes 393224 | tf_op jit(solution)/shard_map/ppermute | solution.py:323
  42.0 4.5 %collective-permute-start.1 = (bf16[16,32,128]{2,1,0:T(8,128)(2,1)S(1)}, bf16[16,32,128]{2,1,0:T(8,128)(2,1)S(1)}, u32[]{:S(2)}, u32[]{:S(2)}) collective-permute-start(bf16[16,32,128]{2,1,0:T(8,128)(2,1)S(1)} %all-to-all-done.mine), channel_id=1, source_target_pairs={{33,0},{32,1},{35,2},{34,3},{37,4},{36,5},{39,6},{38,7},{41,8},{40... | collective-permute-start | bytes 393224 | tf_op jit(solution)/shard_map/ppermute | solution.py:323
  46.5 3.6 %collective-permute-start.2 = (bf16[16,32,128]{2,1,0:T(8,128)(2,1)S(1)}, bf16[16,32,128]{2,1,0:T(8,128)(2,1)S(1)}, u32[]{:S(2)}, u32[]{:S(2)}) collective-permute-start(bf16[16,32,128]{2,1,0:T(8,128)(2,1)S(1)} %all-to-all-done.mine), channel_id=1, source_target_pairs={{32,0},{33,1},{34,2},{35,3},{36,4},{37,5},{38,6},{39,7},{40,8},{41... | collective-permute-start | bytes 393224 | tf_op jit(solution)/shard_map/ppermute | solution.py:323
  50.1 5.8 %all-to-all-done.1.payload = bf16[16,272,128]{2,1,0:T(8,128)(2,1)S(1)} async-done(((bf16[16,272,128]{2,1,0:T(8,128)(2,1)}), bf16[16,272,128]{2,1,0:T(8,128)(2,1)S(1)}, u32[]{:S(2)}, u32[]{:S(2)}) %all-to-all-start.1) | async-done | bytes 1114144 | tf_op jit(solution)/shard_map/all_to_all | solution.py:352
  55.9 0.5 collective-permute-done.other
  56.4 0.9 collective-permute-done.1.other_next
  57.4 0.0 collective-permute-done.2.mine_next
  57.4 0.0 copy-done
  57.4 5.0 %local_gradient.1 = (bf16[32,32,128]{2,1,0:T(8,128)(2,1)S(1)}, bf16[32,32,128]{2,1,0:T(8,128)(2,1)S(1)}) custom-call(s32[1]{0:T(128)} %bitcast.here, s32[16,128]{1,0:T(8,128)S(1)} %bitcast.12, bf16[16,272,128]{2,1,0:T(8,128)(2,1)S(1)} %all-to-all-done.1.payload, bf16[16,32,128]{2,1,0:T(8,128)(2,1)S(1)} %all-to-all-done.mine, ...), custom_call_target="tpu_custom_call" | custom-call | tf_op jit(solution)/shard_map/local_gradient/pallas_call | solution.py:294
  62.4 5.3 %collective-permute-start.3 = (bf16[32,32,128]{2,1,0:T(8,128)(2,1)S(1)}, bf16[32,32,128]{2,1,0:T(8,128)(2,1)S(1)}, u32[]{:S(2)}, u32[]{:S(2)}) collective-permute-start(bf16[32,32,128]{2,1,0:T(8,128)(2,1)S(1)} %get-tuple-element.9), channel_id=1, source_target_pairs={{0,32},{1,33},{2,34},{3,35},{4,36},{5,37},{6,38},{7,39},{8,40},{9,... | collective-permute-start | bytes 786440 | tf_op jit(solution)/shard_map/ppermute | solution.py:323
  67.7 4.7 %collective-permute-done.3 = bf16[32,32,128]{2,1,0:T(8,128)(2,1)S(1)} collective-permute-done((bf16[32,32,128]{2,1,0:T(8,128)(2,1)S(1)}, bf16[32,32,128]{2,1,0:T(8,128)(2,1)S(1)}, u32[]{:S(2)}, u32[]{:S(2)}) %collective-permute-start.3) | collective-permute-done | bytes 262176 | tf_op jit(solution)/shard_map/ppermute | solution.py:323
  72.5 0.1 add_convert_fusion
  72.6 29.9 %all_to_all.15 = bf16[32,32,128]{2,1,0:T(8,128)(2,1)S(1)} all-to-all(bf16[32,32,128]{2,1,0:T(8,128)(2,1)S(1)} %add_convert_fusion), channel_id=1, replica_groups=mesh['tile'=16,'pos'=32] {'pos'}, dimensions={0} | all-to-all | bytes 524288 | tf_op jit(solution)/shard_map/all_to_all | solution.py:365
  102.5 0.6 slice_bitcast_fusion
  (4 shorter events, 0.1 us)
Async XLA Ops:
  2.0 29.9 %all-to-all-start = ((bf16[16,32,128]{2,1,0:T(8,128)(2,1)}), bf16[16,32,128]{2,1,0:T(8,128)(2,1)S(1)}, u32[]{:S(2)}, u32[]{:S(2)}) async-start(bf16[16,32,128]{2,1,0:T(8,128)(2,1)} %spread.1), calls=%async_computation | async-start | bytes 262144 | tf_op jit(solution)/shard_map/all_to_all | solution.py:337
  19.5 19.9 %copy-start.1 = (f32[128,128]{1,0:T(8,128)S(1)}, f32[128,128]{1,0:T(8,128)}, u32[]{:S(2)}) copy-start(f32[128,128]{1,0:T(8,128)} %param.16) | copy-start | bytes 196612
  19.5 19.9 %copy-start.2 = (f32[128,128]{1,0:T(8,128)S(1)}, f32[128,128]{1,0:T(8,128)}, u32[]{:S(2)}) copy-start(f32[128,128]{1,0:T(8,128)} %param.15) | copy-start | bytes 196612
  19.5 37.9 %copy-start = (bf16[4,256,256]{2,1,0:T(8,128)(2,1)S(1)}, bf16[4,256,256]{2,1,0:T(8,128)(2,1)}, u32[]{:S(2)}) copy-start(bf16[4,256,256]{2,1,0:T(8,128)(2,1)} %constant.23.clone.tables) | copy-start | bytes 1572868
  31.9 24.0 %all-to-all-start.1 = ((bf16[16,272,128]{2,1,0:T(8,128)(2,1)}), bf16[16,272,128]{2,1,0:T(8,128)(2,1)S(1)}, u32[]{:S(2)}, u32[]{:S(2)}) async-start(bf16[16,272,128]{2,1,0:T(8,128)(2,1)} %pack.1), calls=%async_computation.1 | async-start | bytes 2228224 | tf_op jit(solution)/shard_map/all_to_all | solution.py:352
  39.4 17.1 %collective-permute-start = (bf16[16,32,128]{2,1,0:T(8,128)(2,1)S(1)}, bf16[16,32,128]{2,1,0:T(8,128)(2,1)S(1)}, u32[]{:S(2)}, u32[]{:S(2)}) collective-permute-start(bf16[16,32,128]{2,1,0:T(8,128)(2,1)S(1)} %all-to-all-done.mine), channel_id=1, source_target_pairs={{1,0},{0,1},{3,2},{2,3},{5,4},{4,5},{7,6},{6,7},{9,8},{8,9},{11,10... | collective-permute-start | bytes 393224 | tf_op jit(solution)/shard_map/ppermute | solution.py:323
  42.0 15.4 %collective-permute-start.1 = (bf16[16,32,128]{2,1,0:T(8,128)(2,1)S(1)}, bf16[16,32,128]{2,1,0:T(8,128)(2,1)S(1)}, u32[]{:S(2)}, u32[]{:S(2)}) collective-permute-start(bf16[16,32,128]{2,1,0:T(8,128)(2,1)S(1)} %all-to-all-done.mine), channel_id=1, source_target_pairs={{33,0},{32,1},{35,2},{34,3},{37,4},{36,5},{39,6},{38,7},{41,8},{40... | collective-permute-start | bytes 393224 | tf_op jit(solution)/shard_map/ppermute | solution.py:323
  46.5 10.9 %collective-permute-start.2 = (bf16[16,32,128]{2,1,0:T(8,128)(2,1)S(1)}, bf16[16,32,128]{2,1,0:T(8,128)(2,1)S(1)}, u32[]{:S(2)}, u32[]{:S(2)}) collective-permute-start(bf16[16,32,128]{2,1,0:T(8,128)(2,1)S(1)} %all-to-all-done.mine), channel_id=1, source_target_pairs={{32,0},{33,1},{34,2},{35,3},{36,4},{37,5},{38,6},{39,7},{40,8},{41... | collective-permute-start | bytes 393224 | tf_op jit(solution)/shard_map/ppermute | solution.py:323
  62.4 10.1 %collective-permute-start.3 = (bf16[32,32,128]{2,1,0:T(8,128)(2,1)S(1)}, bf16[32,32,128]{2,1,0:T(8,128)(2,1)S(1)}, u32[]{:S(2)}, u32[]{:S(2)}) collective-permute-start(bf16[32,32,128]{2,1,0:T(8,128)(2,1)S(1)} %get-tuple-element.9), channel_id=1, source_target_pairs={{0,32},{1,33},{2,34},{3,35},{4,36},{5,37},{6,38},{7,39},{8,40},{9,... | collective-permute-start | bytes 786440 | tf_op jit(solution)/shard_map/ppermute | solution.py:323

commit v6 on v5

--- a/solution.py
+++ b/solution.py
@@ -102,8 +102,10 @@
     mine_next,
     tables,
     probe,
-    own_out,
-    spill_out,
+    own_kept,
+    own_given,
+    spill_kept,
+    spill_given,
     slab,
     acc,
     order,
@@ -274,28 +276,33 @@
 
     lax.fori_loop(0, (n_live + BATCH - 1) // BATCH, run_batch, 0)
 
-    def emit(p, carry):
-        at = pl.multiple_of(p * strip, 8)
-        for a in range(4):
-            for h, ref in enumerate((own_out, spill_out)):
-                ref[p, a * strip : (a + 1) * strip, :] = acc[a, h, pl.ds(at, strip), :].astype(bf16)
+    def emit(z, carry):
+        for ref, y, h in (
+            (own_kept, here[0], 0),
+            (own_given, 1 - here[0], 0),
+            (spill_kept, here[0], 1),
+            (spill_given, 1 - here[0], 1),
+        ):
+            at = pl.multiple_of((2 * z + y) * strip, 8)
+            for a in range(4):
+                ref[z, a * strip : (a + 1) * strip, :] = acc[a, h, pl.ds(at, strip), :].astype(bf16)
         return carry
 
-    lax.fori_loop(0, own_out.shape[0], emit, 0, unroll=4)
+    lax.fori_loop(0, own_kept.shape[0], emit, 0, unroll=4)
 
 
 def local_gradient(here, meta, payload, strips, tables, probe, cap):
     edge = probe.shape[1]
     n_pos = 2 * strips[0].shape[0]
     rows = n_pos * strips[0].shape[1] // 4
-    share = jax.ShapeDtypeStruct((n_pos, *strips[0].shape[1:]), jnp.bfloat16)
+    share = jax.ShapeDtypeStruct(strips[0].shape, jnp.bfloat16)
     smem = pl.BlockSpec(memory_space=pltpu.SMEM)
     vmem = pl.BlockSpec(memory_space=pltpu.VMEM)
     return pl.pallas_call(
         functools.partial(grad_kernel, cap=cap),
-        out_shape=(share, share),
+        out_shape=(share,) * 4,
         in_specs=[smem, smem, vmem, vmem, vmem, vmem, vmem, vmem, vmem],
-        out_specs=(vmem, vmem),
+        out_specs=(vmem,) * 4,
         scratch_shapes=[
             pltpu.VMEM((4, 2, rows, edge), jnp.float32),
             pltpu.VMEM((4, 2, rows, edge), jnp.float32),
@@ -352,7 +359,7 @@
     payload = lax.all_to_all(payload, "tile", 0, 0, tiled=True)
     meta = payload[:, cap * edge_len, :].astype(jnp.int32)
 
-    own, spill = local_gradient(
+    own_kept, own_given, spill_kept, spill_given = local_gradient(
         (lax.axis_index("pos") % 2).astype(jnp.int32).reshape(1),
         meta,
         payload,
@@ -361,8 +368,13 @@
         jnp.stack([probe_real, probe_imag]),
         cap,
     )
-    total = own.astype(jnp.float32) + moved(spill, -1, False).astype(jnp.float32)
-    pieces = lax.all_to_all(total.astype(jnp.bfloat16), "pos", 0, 0, tiled=True)
+    total = own_kept.astype(jnp.float32)
+    total += moved(own_given, 0, True).astype(jnp.float32)
+    total += moved(spill_given, -1, True).astype(jnp.float32)
+    total += moved(spill_kept, -1, False).astype(jnp.float32)
+    pieces = lax.all_to_all(
+        total.astype(jnp.bfloat16), "pos", 0, 0, axis_index_groups=same_y, tiled=True
+    )
     share = jnp.sum(pieces.astype(jnp.float32), axis=0)
     share = share * (1.0 / math.sqrt(per_source * n_pos))
     share = share.reshape(2, slices, strip, tile_width)

time: 104 us -> 102 us (0.981)
  blocking collectives: 29.9 us -> 18.7 us
  starting transfers between devices: 38.7 us -> 44.2 us
  Pallas kernels: 8.64 us -> 12.5 us
    all_to_all x1, blocking collectives: 29.9 us -> 18.7 us  [body(): lax.all_to_all(total.astype(jnp.bfloat16), 'pos', 0, 0, axis_index_groups...]
    ppermute x4 -> x6, starting transfers between devices: 16.1 us -> 21.6 us  [moved(): return lax.ppermute(value, ('tile', 'pos'), pairs)]
    pallas_call x1, Pallas kernels: 5.01 us -> 8.86 us  [local_gradient(): pl.pallas_call(functools.partial(grad_kernel, cap=cap), out_shape=(share,...]
    ppermute x4 -> x6, waiting for transfers between devices: 6.16 us -> 6.35 us  [moved(): return lax.ppermute(value, ('tile', 'pos'), pairs)]
  transfers between devices with their start and end apart: 6 -> 8, of which waited for: 5 -> 6; matrix products, arithmetic and copies ran while one was open for 0% -> 0% of each run, Pallas kernels for 2% -> 2%
where the time goes in v6:
time: 102 us
  starting transfers between devices  44.2 us (43%)
  waiting for transfers between devices  24.6 us (24%)
  blocking collectives  18.7 us (18%)
  Pallas kernels  12.5 us (12%)
    ppermute x6, starting transfers between devices, moved(): return lax.ppermute(value, ('tile', 'pos'), pairs)  21.6 us
    all_to_all x1, blocking collectives, body(): lax.all_to_all(total.astype(jnp.bfloat16), 'pos', 0, 0, axis_index_groups...  18.7 us
    all_to_all x1, starting transfers between devices, body(): lax.all_to_all(sent, 'pos', 0, 0, axis_index_groups=same_y, tiled=True)  15.2 us
    all_to_all x1, waiting for transfers between devices, body(): lax.all_to_all(sent, 'pos', 0, 0, axis_index_groups=same_y, tiled=True)  12.4 us
    pallas_call x1, Pallas kernels, local_gradient(): pl.pallas_call(functools.partial(grad_kernel, cap=cap), out_shape=(share,...  8.86 us
    all_to_all x1, starting transfers between devices, body(): payload = lax.all_to_all(payload, 'tile', 0, 0, tiled=True)  7.43 us
    ppermute x6, waiting for transfers between devices, moved(): return lax.ppermute(value, ('tile', 'pos'), pairs)  6.35 us
    all_to_all x1, waiting for transfers between devices, body(): payload = lax.all_to_all(payload, 'tile', 0, 0, tiled=True)  5.81 us
  transfers between devices with their start and end apart: 8, of which 6 were waited for; matrix products, arithmetic and copies ran while one was open for 0% of the time, Pallas kernels for 2%

profile of v6, /device:TPU:6, one launch (start us, length us, event | category | flops | bytes accessed | tf_op | source)
XLA Modules:
  0.0 101.5 jit_solution(11043016685907902260)
XLA Ops:
  0.6 1.4 %spread.1 = bf16[16,32,128]{2,1,0:T(8,128)(2,1)} custom-call(f32[2,8,128]{2,1,0:T(8,128)} %real.1, f32[2,8,128]{2,1,0:T(8,128)} %imag.1), custom_call_target="tpu_custom_call" | custom-call | tf_op jit(solution)/shard_map/spread/pallas_call | solution.py:53
  2.0 15.2 %all-to-all-start = ((bf16[16,32,128]{2,1,0:T(8,128)(2,1)}), bf16[16,32,128]{2,1,0:T(8,128)(2,1)S(1)}, u32[]{:S(2)}, u32[]{:S(2)}) async-start(bf16[16,32,128]{2,1,0:T(8,128)(2,1)} %spread.1), calls=%async_computation | async-start | bytes 262144 | tf_op jit(solution)/shard_map/all_to_all | solution.py:344
  17.2 2.3 %pack.1 = bf16[16,272,128]{2,1,0:T(8,128)(2,1)} custom-call(s32[2,16]{1,0:T(2,128)} %bitcast.15, s32[1,16]{1,0:T(1,128)} %counts.1, s32[2,16]{1,0:T(2,128)} %bitcast.16, bf16[16,128,128]{2,1,0:T(8,128)(2,1)} %patterns.1), custom_call_target="tpu_custom_call" | custom-call | tf_op jit(solution)/shard_map/pack/pallas_call | solution.py:86
  19.5 0.0 copy-start.1
  19.5 0.0 copy-start.2
  19.5 0.0 copy-start
  19.5 12.4 %all-to-all-done.mine = bf16[16,32,128]{2,1,0:T(8,128)(2,1)S(1)} async-done(((bf16[16,32,128]{2,1,0:T(8,128)(2,1)}), bf16[16,32,128]{2,1,0:T(8,128)(2,1)S(1)}, u32[]{:S(2)}, u32[]{:S(2)}) %all-to-all-start) | async-done | bytes 131104 | tf_op jit(solution)/shard_map/all_to_all | solution.py:344
  31.9 7.4 %all-to-all-start.1 = ((bf16[16,272,128]{2,1,0:T(8,128)(2,1)}), bf16[16,272,128]{2,1,0:T(8,128)(2,1)S(1)}, u32[]{:S(2)}, u32[]{:S(2)}) async-start(bf16[16,272,128]{2,1,0:T(8,128)(2,1)} %pack.1), calls=%async_computation.1 | async-start | bytes 2228224 | tf_op jit(solution)/shard_map/all_to_all | solution.py:359
  39.3 0.0 copy-done.1
  39.3 0.0 copy-done.2
  39.4 2.6 %collective-permute-start = (bf16[16,32,128]{2,1,0:T(8,128)(2,1)S(1)}, bf16[16,32,128]{2,1,0:T(8,128)(2,1)S(1)}, u32[]{:S(2)}, u32[]{:S(2)}) collective-permute-start(bf16[16,32,128]{2,1,0:T(8,128)(2,1)S(1)} %all-to-all-done.mine), channel_id=1, source_target_pairs={{1,0},{0,1},{3,2},{2,3},{5,4},{4,5},{7,6},{6,7},{9,8},{8,9},{11,10... | collective-permute-start | bytes 393224 | tf_op jit(solution)/shard_map/ppermute | solution.py:330
  42.0 4.5 %collective-permute-start.1 = (bf16[16,32,128]{2,1,0:T(8,128)(2,1)S(1)}, bf16[16,32,128]{2,1,0:T(8,128)(2,1)S(1)}, u32[]{:S(2)}, u32[]{:S(2)}) collective-permute-start(bf16[16,32,128]{2,1,0:T(8,128)(2,1)S(1)} %all-to-all-done.mine), channel_id=1, source_target_pairs={{33,0},{32,1},{35,2},{34,3},{37,4},{36,5},{39,6},{38,7},{41,8},{40... | collective-permute-start | bytes 393224 | tf_op jit(solution)/shard_map/ppermute | solution.py:330
  46.5 3.6 %collective-permute-start.2 = (bf16[16,32,128]{2,1,0:T(8,128)(2,1)S(1)}, bf16[16,32,128]{2,1,0:T(8,128)(2,1)S(1)}, u32[]{:S(2)}, u32[]{:S(2)}) collective-permute-start(bf16[16,32,128]{2,1,0:T(8,128)(2,1)S(1)} %all-to-all-done.mine), channel_id=1, source_target_pairs={{32,0},{33,1},{34,2},{35,3},{36,4},{37,5},{38,6},{39,7},{40,8},{41... | collective-permute-start | bytes 393224 | tf_op jit(solution)/shard_map/ppermute | solution.py:330
  50.1 5.8 %all-to-all-done.1.payload = bf16[16,272,128]{2,1,0:T(8,128)(2,1)S(1)} async-done(((bf16[16,272,128]{2,1,0:T(8,128)(2,1)}), bf16[16,272,128]{2,1,0:T(8,128)(2,1)S(1)}, u32[]{:S(2)}, u32[]{:S(2)}) %all-to-all-start.1) | async-done | bytes 1114144 | tf_op jit(solution)/shard_map/all_to_all | solution.py:359
  55.9 0.5 collective-permute-done.other
  56.4 0.9 collective-permute-done.1.other_next
  57.4 0.0 collective-permute-done.2.mine_next
  57.4 0.0 copy-done
  57.4 8.9 %local_gradient.1 = (bf16[16,32,128]{2,1,0:T(8,128)(2,1)S(1)}, bf16[16,32,128]{2,1,0:T(8,128)(2,1)S(1)}, bf16[16,32,128]{2,1,0:T(8,128)(2,1)S(1)}, bf16[16,32,128]{2,1,0:T(8,128)(2,1)S(1)}) custom-call(s32[1]{0:T(128)} %bitcast.here, s32[16,128]{1,0:T(8,128)S(1)} %bitcast.12, bf16[16,272,128]{2,1,0:T(8,128)(2,1)S(1)} %all-to-all-done.1.payload, ...), custom_call_target="tpu_custom_call" | custom-call | tf_op jit(solution)/shard_map/local_gradient/pallas_call | solution.py:301
  66.2 1.9 %collective-permute-start.5 = (bf16[16,32,128]{2,1,0:T(8,128)(2,1)S(1)}, bf16[16,32,128]{2,1,0:T(8,128)(2,1)S(1)}, u32[]{:S(2)}, u32[]{:S(2)}) collective-permute-start(bf16[16,32,128]{2,1,0:T(8,128)(2,1)S(1)} %get-tuple-element.13), channel_id=1, source_target_pairs={{0,32},{1,33},{2,34},{3,35},{4,36},{5,37},{6,38},{7,39},{8,40},{9,... | collective-permute-start | bytes 393224 | tf_op jit(solution)/shard_map/ppermute | solution.py:330
  68.2 7.0 %collective-permute-start.4 = (bf16[16,32,128]{2,1,0:T(8,128)(2,1)S(1)}, bf16[16,32,128]{2,1,0:T(8,128)(2,1)S(1)}, u32[]{:S(2)}, u32[]{:S(2)}) collective-permute-start(bf16[16,32,128]{2,1,0:T(8,128)(2,1)S(1)} %get-tuple-element.12), channel_id=1, source_target_pairs={{1,32},{0,33},{3,34},{2,35},{5,36},{4,37},{7,38},{6,39},{9,40},{8,... | collective-permute-start | bytes 393224 | tf_op jit(solution)/shard_map/ppermute | solution.py:330
  75.2 1.9 %collective-permute-start.3 = (bf16[16,32,128]{2,1,0:T(8,128)(2,1)S(1)}, bf16[16,32,128]{2,1,0:T(8,128)(2,1)S(1)}, u32[]{:S(2)}, u32[]{:S(2)}) collective-permute-start(bf16[16,32,128]{2,1,0:T(8,128)(2,1)S(1)} %get-tuple-element.11), channel_id=1, source_target_pairs={{1,0},{0,1},{3,2},{2,3},{5,4},{4,5},{7,6},{6,7},{9,8},{8,9},{11,10... | collective-permute-start | bytes 393224 | tf_op jit(solution)/shard_map/ppermute | solution.py:330
  77.1 0.0 collective-permute-done.5
  77.2 0.6 collective-permute-done.4
  77.7 4.4 %collective-permute-done.3 = bf16[16,32,128]{2,1,0:T(8,128)(2,1)S(1)} collective-permute-done((bf16[16,32,128]{2,1,0:T(8,128)(2,1)S(1)}, bf16[16,32,128]{2,1,0:T(8,128)(2,1)S(1)}, u32[]{:S(2)}, u32[]{:S(2)}) %collective-permute-start.3) | collective-permute-done | bytes 131104 | tf_op jit(solution)/shard_map/ppermute | solution.py:330
  82.1 0.1 add_convert_fusion
  82.2 18.7 %all_to_all.15 = bf16[16,32,128]{2,1,0:T(8,128)(2,1)S(1)} all-to-all(bf16[16,32,128]{2,1,0:T(8,128)(2,1)S(1)} %add_convert_fusion), channel_id=1, replica_groups={{0,2,4,6,8,10,12,14,16,18,20,22,24,26,28,30},{1,3,5,7,9,11,13,15,17,19,..., dimensions={0} | all-to-all | bytes 262144 | tf_op jit(solution)/shard_map/all_to_all | solution.py:375
  100.9 0.6 slice_bitcast_fusion
  (4 shorter events, 0.0 us)
Async XLA Ops:
  2.0 29.9 %all-to-all-start = ((bf16[16,32,128]{2,1,0:T(8,128)(2,1)}), bf16[16,32,128]{2,1,0:T(8,128)(2,1)S(1)}, u32[]{:S(2)}, u32[]{:S(2)}) async-start(bf16[16,32,128]{2,1,0:T(8,128)(2,1)} %spread.1), calls=%async_computation | async-start | bytes 262144 | tf_op jit(solution)/shard_map/all_to_all | solution.py:344
  19.5 19.9 %copy-start.1 = (f32[128,128]{1,0:T(8,128)S(1)}, f32[128,128]{1,0:T(8,128)}, u32[]{:S(2)}) copy-start(f32[128,128]{1,0:T(8,128)} %param.16) | copy-start | bytes 196612
  19.5 19.9 %copy-start.2 = (f32[128,128]{1,0:T(8,128)S(1)}, f32[128,128]{1,0:T(8,128)}, u32[]{:S(2)}) copy-start(f32[128,128]{1,0:T(8,128)} %param.15) | copy-start | bytes 196612
  19.5 37.9 %copy-start = (bf16[4,256,256]{2,1,0:T(8,128)(2,1)S(1)}, bf16[4,256,256]{2,1,0:T(8,128)(2,1)}, u32[]{:S(2)}) copy-start(bf16[4,256,256]{2,1,0:T(8,128)(2,1)} %constant.23.clone.tables) | copy-start | bytes 1572868
  31.9 24.0 %all-to-all-start.1 = ((bf16[16,272,128]{2,1,0:T(8,128)(2,1)}), bf16[16,272,128]{2,1,0:T(8,128)(2,1)S(1)}, u32[]{:S(2)}, u32[]{:S(2)}) async-start(bf16[16,272,128]{2,1,0:T(8,128)(2,1)} %pack.1), calls=%async_computation.1 | async-start | bytes 2228224 | tf_op jit(solution)/shard_map/all_to_all | solution.py:359
  39.4 17.1 %collective-permute-start = (bf16[16,32,128]{2,1,0:T(8,128)(2,1)S(1)}, bf16[16,32,128]{2,1,0:T(8,128)(2,1)S(1)}, u32[]{:S(2)}, u32[]{:S(2)}) collective-permute-start(bf16[16,32,128]{2,1,0:T(8,128)(2,1)S(1)} %all-to-all-done.mine), channel_id=1, source_target_pairs={{1,0},{0,1},{3,2},{2,3},{5,4},{4,5},{7,6},{6,7},{9,8},{8,9},{11,10... | collective-permute-start | bytes 393224 | tf_op jit(solution)/shard_map/ppermute | solution.py:330
  42.0 15.4 %collective-permute-start.1 = (bf16[16,32,128]{2,1,0:T(8,128)(2,1)S(1)}, bf16[16,32,128]{2,1,0:T(8,128)(2,1)S(1)}, u32[]{:S(2)}, u32[]{:S(2)}) collective-permute-start(bf16[16,32,128]{2,1,0:T(8,128)(2,1)S(1)} %all-to-all-done.mine), channel_id=1, source_target_pairs={{33,0},{32,1},{35,2},{34,3},{37,4},{36,5},{39,6},{38,7},{41,8},{40... | collective-permute-start | bytes 393224 | tf_op jit(solution)/shard_map/ppermute | solution.py:330
  46.5 10.9 %collective-permute-start.2 = (bf16[16,32,128]{2,1,0:T(8,128)(2,1)S(1)}, bf16[16,32,128]{2,1,0:T(8,128)(2,1)S(1)}, u32[]{:S(2)}, u32[]{:S(2)}) collective-permute-start(bf16[16,32,128]{2,1,0:T(8,128)(2,1)S(1)} %all-to-all-done.mine), channel_id=1, source_target_pairs={{32,0},{33,1},{34,2},{35,3},{36,4},{37,5},{38,6},{39,7},{40,8},{41... | collective-permute-start | bytes 393224 | tf_op jit(solution)/shard_map/ppermute | solution.py:330
  66.2 10.9 %collective-permute-start.5 = (bf16[16,32,128]{2,1,0:T(8,128)(2,1)S(1)}, bf16[16,32,128]{2,1,0:T(8,128)(2,1)S(1)}, u32[]{:S(2)}, u32[]{:S(2)}) collective-permute-start(bf16[16,32,128]{2,1,0:T(8,128)(2,1)S(1)} %get-tuple-element.13), channel_id=1, source_target_pairs={{0,32},{1,33},{2,34},{3,35},{4,36},{5,37},{6,38},{7,39},{8,40},{9,... | collective-permute-start | bytes 393224 | tf_op jit(solution)/shard_map/ppermute | solution.py:330
  68.2 9.5 %collective-permute-start.4 = (bf16[16,32,128]{2,1,0:T(8,128)(2,1)S(1)}, bf16[16,32,128]{2,1,0:T(8,128)(2,1)S(1)}, u32[]{:S(2)}, u32[]{:S(2)}) collective-permute-start(bf16[16,32,128]{2,1,0:T(8,128)(2,1)S(1)} %get-tuple-element.12), channel_id=1, source_target_pairs={{1,32},{0,33},{3,34},{2,35},{5,36},{4,37},{7,38},{6,39},{9,40},{8,... | collective-permute-start | bytes 393224 | tf_op jit(solution)/shard_map/ppermute | solution.py:330
  75.2 6.9 %collective-permute-start.3 = (bf16[16,32,128]{2,1,0:T(8,128)(2,1)S(1)}, bf16[16,32,128]{2,1,0:T(8,128)(2,1)S(1)}, u32[]{:S(2)}, u32[]{:S(2)}) collective-permute-start(bf16[16,32,128]{2,1,0:T(8,128)(2,1)S(1)} %get-tuple-element.11), channel_id=1, source_target_pairs={{1,0},{0,1},{3,2},{2,3},{5,4},{4,5},{7,6},{6,7},{9,8},{8,9},{11,10... | collective-permute-start | bytes 393224 | tf_op jit(solution)/shard_map/ppermute | solution.py:330

commit v7 on v6

--- a/solution.py
+++ b/solution.py
@@ -369,9 +369,9 @@
         cap,
     )
     total = own_kept.astype(jnp.float32)
+    total += moved(spill_kept, -1, False).astype(jnp.float32)
+    total += moved(spill_given, -1, True).astype(jnp.float32)
     total += moved(own_given, 0, True).astype(jnp.float32)
-    total += moved(spill_given, -1, True).astype(jnp.float32)
-    total += moved(spill_kept, -1, False).astype(jnp.float32)
     pieces = lax.all_to_all(
         total.astype(jnp.bfloat16), "pos", 0, 0, axis_index_groups=same_y, tiled=True
     )

time: 102 us -> 102 us (level)
  blocking collectives: 18.7 us -> 16.7 us
  waiting for transfers between devices: 24.6 us -> 26.4 us
    all_to_all x1, blocking collectives: 18.7 us -> 16.7 us  [body(): lax.all_to_all(total.astype(jnp.bfloat16), 'pos', 0, 0, axis_index_groups...]
    ppermute x6, waiting for transfers between devices: 6.35 us -> 8.18 us  [moved(): return lax.ppermute(value, ('tile', 'pos'), pairs)]
where the time goes in v7:
time: 102 us; the launch traced here: 101 us
  starting transfers between devices  44.4 us (44%)
  waiting for transfers between devices  26.4 us (26%)
  blocking collectives  16.7 us (16%)
  Pallas kernels  12.3 us (12%)
    ppermute x6, starting transfers between devices, moved(): return lax.ppermute(value, ('tile', 'pos'), pairs)  21.8 us
    all_to_all x1, blocking collectives, body(): lax.all_to_all(total.astype(jnp.bfloat16), 'pos', 0, 0, axis_index_groups...  16.7 us
    all_to_all x1, starting transfers between devices, body(): lax.all_to_all(sent, 'pos', 0, 0, axis_index_groups=same_y, tiled=True)  15.2 us
    all_to_all x1, waiting for transfers between devices, body(): lax.all_to_all(sent, 'pos', 0, 0, axis_index_groups=same_y, tiled=True)  12.4 us
    pallas_call x1, Pallas kernels, local_gradient(): pl.pallas_call(functools.partial(grad_kernel, cap=cap), out_shape=(share,...  8.62 us
    ppermute x6, waiting for transfers between devices, moved(): return lax.ppermute(value, ('tile', 'pos'), pairs)  8.18 us
    all_to_all x1, starting transfers between devices, body(): payload = lax.all_to_all(payload, 'tile', 0, 0, tiled=True)  7.43 us
    all_to_all x1, waiting for transfers between devices, body(): payload = lax.all_to_all(payload, 'tile', 0, 0, tiled=True)  5.81 us
  transfers between devices with their start and end apart: 8, of which 6 were waited for; matrix products, arithmetic and copies ran while one was open for 0% of the time, Pallas kernels for 2%

profile of v7, /device:TPU:6, one launch (start us, length us, event | category | flops | bytes accessed | tf_op | source)
XLA Modules:
  0.0 101.3 jit_solution(13757200500147785840)
XLA Ops:
  0.6 1.4 %spread.1 = bf16[16,32,128]{2,1,0:T(8,128)(2,1)} custom-call(f32[2,8,128]{2,1,0:T(8,128)} %real.1, f32[2,8,128]{2,1,0:T(8,128)} %imag.1), custom_call_target="tpu_custom_call" | custom-call | tf_op jit(solution)/shard_map/spread/pallas_call | solution.py:53
  2.0 15.2 %all-to-all-start = ((bf16[16,32,128]{2,1,0:T(8,128)(2,1)}), bf16[16,32,128]{2,1,0:T(8,128)(2,1)S(1)}, u32[]{:S(2)}, u32[]{:S(2)}) async-start(bf16[16,32,128]{2,1,0:T(8,128)(2,1)} %spread.1), calls=%async_computation | async-start | bytes 262144 | tf_op jit(solution)/shard_map/all_to_all | solution.py:344
  17.2 2.3 %pack.1 = bf16[16,272,128]{2,1,0:T(8,128)(2,1)} custom-call(s32[2,16]{1,0:T(2,128)} %bitcast.15, s32[1,16]{1,0:T(1,128)} %counts.1, s32[2,16]{1,0:T(2,128)} %bitcast.16, bf16[16,128,128]{2,1,0:T(8,128)(2,1)} %patterns.1), custom_call_target="tpu_custom_call" | custom-call | tf_op jit(solution)/shard_map/pack/pallas_call | solution.py:86
  19.5 0.0 copy-start.1
  19.5 0.0 copy-start.2
  19.5 0.0 copy-start
  19.5 12.4 %all-to-all-done.mine = bf16[16,32,128]{2,1,0:T(8,128)(2,1)S(1)} async-done(((bf16[16,32,128]{2,1,0:T(8,128)(2,1)}), bf16[16,32,128]{2,1,0:T(8,128)(2,1)S(1)}, u32[]{:S(2)}, u32[]{:S(2)}) %all-to-all-start) | async-done | bytes 131104 | tf_op jit(solution)/shard_map/all_to_all | solution.py:344
  31.9 7.4 %all-to-all-start.1 = ((bf16[16,272,128]{2,1,0:T(8,128)(2,1)}), bf16[16,272,128]{2,1,0:T(8,128)(2,1)S(1)}, u32[]{:S(2)}, u32[]{:S(2)}) async-start(bf16[16,272,128]{2,1,0:T(8,128)(2,1)} %pack.1), calls=%async_computation.1 | async-start | bytes 2228224 | tf_op jit(solution)/shard_map/all_to_all | solution.py:359
  39.3 0.0 copy-done.1
  39.3 0.0 copy-done.2
  39.4 2.6 %collective-permute-start = (bf16[16,32,128]{2,1,0:T(8,128)(2,1)S(1)}, bf16[16,32,128]{2,1,0:T(8,128)(2,1)S(1)}, u32[]{:S(2)}, u32[]{:S(2)}) collective-permute-start(bf16[16,32,128]{2,1,0:T(8,128)(2,1)S(1)} %all-to-all-done.mine), channel_id=1, source_target_pairs={{1,0},{0,1},{3,2},{2,3},{5,4},{4,5},{7,6},{6,7},{9,8},{8,9},{11,10... | collective-permute-start | bytes 393224 | tf_op jit(solution)/shard_map/ppermute | solution.py:330
  42.0 4.5 %collective-permute-start.1 = (bf16[16,32,128]{2,1,0:T(8,128)(2,1)S(1)}, bf16[16,32,128]{2,1,0:T(8,128)(2,1)S(1)}, u32[]{:S(2)}, u32[]{:S(2)}) collective-permute-start(bf16[16,32,128]{2,1,0:T(8,128)(2,1)S(1)} %all-to-all-done.mine), channel_id=1, source_target_pairs={{33,0},{32,1},{35,2},{34,3},{37,4},{36,5},{39,6},{38,7},{41,8},{40... | collective-permute-start | bytes 393224 | tf_op jit(solution)/shard_map/ppermute | solution.py:330
  46.5 3.6 %collective-permute-start.2 = (bf16[16,32,128]{2,1,0:T(8,128)(2,1)S(1)}, bf16[16,32,128]{2,1,0:T(8,128)(2,1)S(1)}, u32[]{:S(2)}, u32[]{:S(2)}) collective-permute-start(bf16[16,32,128]{2,1,0:T(8,128)(2,1)S(1)} %all-to-all-done.mine), channel_id=1, source_target_pairs={{32,0},{33,1},{34,2},{35,3},{36,4},{37,5},{38,6},{39,7},{40,8},{41... | collective-permute-start | bytes 393224 | tf_op jit(solution)/shard_map/ppermute | solution.py:330
  50.1 5.8 %all-to-all-done.1.payload = bf16[16,272,128]{2,1,0:T(8,128)(2,1)S(1)} async-done(((bf16[16,272,128]{2,1,0:T(8,128)(2,1)}), bf16[16,272,128]{2,1,0:T(8,128)(2,1)S(1)}, u32[]{:S(2)}, u32[]{:S(2)}) %all-to-all-start.1) | async-done | bytes 1114144 | tf_op jit(solution)/shard_map/all_to_all | solution.py:359
  55.9 0.5 collective-permute-done.other
  56.4 0.9 collective-permute-done.1.other_next
  57.4 0.0 collective-permute-done.2.mine_next
  57.4 0.0 copy-done
  57.4 8.6 %local_gradient.1 = (bf16[16,32,128]{2,1,0:T(8,128)(2,1)S(1)}, bf16[16,32,128]{2,1,0:T(8,128)(2,1)S(1)}, bf16[16,32,128]{2,1,0:T(8,128)(2,1)S(1)}, bf16[16,32,128]{2,1,0:T(8,128)(2,1)S(1)}) custom-call(s32[1]{0:T(128)} %bitcast.here, s32[16,128]{1,0:T(8,128)S(1)} %bitcast.12, bf16[16,272,128]{2,1,0:T(8,128)(2,1)S(1)} %all-to-all-done.1.payload, ...), custom_call_target="tpu_custom_call" | custom-call | tf_op jit(solution)/shard_map/local_gradient/pallas_call | solution.py:301
  66.0 3.6 %collective-permute-start.5 = (bf16[16,32,128]{2,1,0:T(8,128)(2,1)S(1)}, bf16[16,32,128]{2,1,0:T(8,128)(2,1)S(1)}, u32[]{:S(2)}, u32[]{:S(2)}) collective-permute-start(bf16[16,32,128]{2,1,0:T(8,128)(2,1)S(1)} %get-tuple-element.13), channel_id=1, source_target_pairs={{1,0},{0,1},{3,2},{2,3},{5,4},{4,5},{7,6},{6,7},{9,8},{8,9},{11,10... | collective-permute-start | bytes 393224 | tf_op jit(solution)/shard_map/ppermute | solution.py:330
  69.6 5.6 %collective-permute-start.4 = (bf16[16,32,128]{2,1,0:T(8,128)(2,1)S(1)}, bf16[16,32,128]{2,1,0:T(8,128)(2,1)S(1)}, u32[]{:S(2)}, u32[]{:S(2)}) collective-permute-start(bf16[16,32,128]{2,1,0:T(8,128)(2,1)S(1)} %get-tuple-element.12), channel_id=1, source_target_pairs={{1,32},{0,33},{3,34},{2,35},{5,36},{4,37},{7,38},{6,39},{9,40},{8,... | collective-permute-start | bytes 393224 | tf_op jit(solution)/shard_map/ppermute | solution.py:330
  75.1 1.9 %collective-permute-start.3 = (bf16[16,32,128]{2,1,0:T(8,128)(2,1)S(1)}, bf16[16,32,128]{2,1,0:T(8,128)(2,1)S(1)}, u32[]{:S(2)}, u32[]{:S(2)}) collective-permute-start(bf16[16,32,128]{2,1,0:T(8,128)(2,1)S(1)} %get-tuple-element.11), channel_id=1, source_target_pairs={{0,32},{1,33},{2,34},{3,35},{4,36},{5,37},{6,38},{7,39},{8,40},{9,... | collective-permute-start | bytes 393224 | tf_op jit(solution)/shard_map/ppermute | solution.py:330
  77.1 0.0 collective-permute-done.5
  77.1 0.9 collective-permute-done.4
  78.0 5.9 %collective-permute-done.3 = bf16[16,32,128]{2,1,0:T(8,128)(2,1)S(1)} collective-permute-done((bf16[16,32,128]{2,1,0:T(8,128)(2,1)S(1)}, bf16[16,32,128]{2,1,0:T(8,128)(2,1)S(1)}, u32[]{:S(2)}, u32[]{:S(2)}) %collective-permute-start.3) | collective-permute-done | bytes 131104 | tf_op jit(solution)/shard_map/ppermute | solution.py:330
  83.8 0.1 add_convert_fusion
  83.9 16.7 %all_to_all.15 = bf16[16,32,128]{2,1,0:T(8,128)(2,1)S(1)} all-to-all(bf16[16,32,128]{2,1,0:T(8,128)(2,1)S(1)} %add_convert_fusion), channel_id=1, replica_groups={{0,2,4,6,8,10,12,14,16,18,20,22,24,26,28,30},{1,3,5,7,9,11,13,15,17,19,..., dimensions={0} | all-to-all | bytes 262144 | tf_op jit(solution)/shard_map/all_to_all | solution.py:375
  100.7 0.6 slice_bitcast_fusion
  (4 shorter events, 0.0 us)
Async XLA Ops:
  2.0 29.9 %all-to-all-start = ((bf16[16,32,128]{2,1,0:T(8,128)(2,1)}), bf16[16,32,128]{2,1,0:T(8,128)(2,1)S(1)}, u32[]{:S(2)}, u32[]{:S(2)}) async-start(bf16[16,32,128]{2,1,0:T(8,128)(2,1)} %spread.1), calls=%async_computation | async-start | bytes 262144 | tf_op jit(solution)/shard_map/all_to_all | solution.py:344
  19.5 19.9 %copy-start.1 = (f32[128,128]{1,0:T(8,128)S(1)}, f32[128,128]{1,0:T(8,128)}, u32[]{:S(2)}) copy-start(f32[128,128]{1,0:T(8,128)} %param.16) | copy-start | bytes 196612
  19.5 19.9 %copy-start.2 = (f32[128,128]{1,0:T(8,128)S(1)}, f32[128,128]{1,0:T(8,128)}, u32[]{:S(2)}) copy-start(f32[128,128]{1,0:T(8,128)} %param.15) | copy-start | bytes 196612
  19.5 37.9 %copy-start = (bf16[4,256,256]{2,1,0:T(8,128)(2,1)S(1)}, bf16[4,256,256]{2,1,0:T(8,128)(2,1)}, u32[]{:S(2)}) copy-start(bf16[4,256,256]{2,1,0:T(8,128)(2,1)} %constant.23.clone.tables) | copy-start | bytes 1572868
  31.9 24.0 %all-to-all-start.1 = ((bf16[16,272,128]{2,1,0:T(8,128)(2,1)}), bf16[16,272,128]{2,1,0:T(8,128)(2,1)S(1)}, u32[]{:S(2)}, u32[]{:S(2)}) async-start(bf16[16,272,128]{2,1,0:T(8,128)(2,1)} %pack.1), calls=%async_computation.1 | async-start | bytes 2228224 | tf_op jit(solution)/shard_map/all_to_all | solution.py:359
  39.4 17.1 %collective-permute-start = (bf16[16,32,128]{2,1,0:T(8,128)(2,1)S(1)}, bf16[16,32,128]{2,1,0:T(8,128)(2,1)S(1)}, u32[]{:S(2)}, u32[]{:S(2)}) collective-permute-start(bf16[16,32,128]{2,1,0:T(8,128)(2,1)S(1)} %all-to-all-done.mine), channel_id=1, source_target_pairs={{1,0},{0,1},{3,2},{2,3},{5,4},{4,5},{7,6},{6,7},{9,8},{8,9},{11,10... | collective-permute-start | bytes 393224 | tf_op jit(solution)/shard_map/ppermute | solution.py:330
  42.0 15.4 %collective-permute-start.1 = (bf16[16,32,128]{2,1,0:T(8,128)(2,1)S(1)}, bf16[16,32,128]{2,1,0:T(8,128)(2,1)S(1)}, u32[]{:S(2)}, u32[]{:S(2)}) collective-permute-start(bf16[16,32,128]{2,1,0:T(8,128)(2,1)S(1)} %all-to-all-done.mine), channel_id=1, source_target_pairs={{33,0},{32,1},{35,2},{34,3},{37,4},{36,5},{39,6},{38,7},{41,8},{40... | collective-permute-start | bytes 393224 | tf_op jit(solution)/shard_map/ppermute | solution.py:330
  46.5 10.9 %collective-permute-start.2 = (bf16[16,32,128]{2,1,0:T(8,128)(2,1)S(1)}, bf16[16,32,128]{2,1,0:T(8,128)(2,1)S(1)}, u32[]{:S(2)}, u32[]{:S(2)}) collective-permute-start(bf16[16,32,128]{2,1,0:T(8,128)(2,1)S(1)} %all-to-all-done.mine), channel_id=1, source_target_pairs={{32,0},{33,1},{34,2},{35,3},{36,4},{37,5},{38,6},{39,7},{40,8},{41... | collective-permute-start | bytes 393224 | tf_op jit(solution)/shard_map/ppermute | solution.py:330
  66.0 11.1 %collective-permute-start.5 = (bf16[16,32,128]{2,1,0:T(8,128)(2,1)S(1)}, bf16[16,32,128]{2,1,0:T(8,128)(2,1)S(1)}, u32[]{:S(2)}, u32[]{:S(2)}) collective-permute-start(bf16[16,32,128]{2,1,0:T(8,128)(2,1)S(1)} %get-tuple-element.13), channel_id=1, source_target_pairs={{1,0},{0,1},{3,2},{2,3},{5,4},{4,5},{7,6},{6,7},{9,8},{8,9},{11,10... | collective-permute-start | bytes 393224 | tf_op jit(solution)/shard_map/ppermute | solution.py:330
  69.6 8.4 %collective-permute-start.4 = (bf16[16,32,128]{2,1,0:T(8,128)(2,1)S(1)}, bf16[16,32,128]{2,1,0:T(8,128)(2,1)S(1)}, u32[]{:S(2)}, u32[]{:S(2)}) collective-permute-start(bf16[16,32,128]{2,1,0:T(8,128)(2,1)S(1)} %get-tuple-element.12), channel_id=1, source_target_pairs={{1,32},{0,33},{3,34},{2,35},{5,36},{4,37},{7,38},{6,39},{9,40},{8,... | collective-permute-start | bytes 393224 | tf_op jit(solution)/shard_map/ppermute | solution.py:330
  75.1 8.7 %collective-permute-start.3 = (bf16[16,32,128]{2,1,0:T(8,128)(2,1)S(1)}, bf16[16,32,128]{2,1,0:T(8,128)(2,1)S(1)}, u32[]{:S(2)}, u32[]{:S(2)}) collective-permute-start(bf16[16,32,128]{2,1,0:T(8,128)(2,1)S(1)} %get-tuple-element.11), channel_id=1, source_target_pairs={{0,32},{1,33},{2,34},{3,35},{4,36},{5,37},{6,38},{7,39},{8,40},{9,... | collective-permute-start | bytes 393224 | tf_op jit(solution)/shard_map/ppermute | solution.py:330
